TPU v7x, 32 devices: a whole 2x2x4 slice. The times are simulated.
32 devices in a mesh: rep: 8 (over z, core), fsdp: 4 (over y, x).
Axes of the slice: x: 2, y: 2, z: 4, core: 2. Of those that a mesh axis runs over, the one named last changes fastest.
Arguments:
- tokens: bfloat16 [8192, 1536], P(('rep', 'fsdp')), may hold values from -6 to 6
- segment_ids: int32 [32, 256], P(('rep', 'fsdp')), may hold values from 0 to 3, never falling along the last dimension, each value on 1 to 128 neighbouring positions
- cotangent: bfloat16 [8192, 1536], P(('rep', 'fsdp')), may hold values from -6 to 6
- norm_gain: bfloat16 [1536], P('fsdp'), may hold values from 0.5 to 1.5
- in_weight: bfloat16 [1536, 6448], P('fsdp'), may hold values from -0.15625 to 0.15625
- conv_weight: bfloat16 [4, 3328], P(None, 'fsdp'), may hold values from -3 to 3
- conv_bias: bfloat16 [3328], P('fsdp'), may hold values from -0.5 to 0.5
- step_bias: bfloat16 [48], replicated, may hold values from -6 to -2
- rate_log: bfloat16 [48], replicated, may hold values from 0 to 2.5
- skip_gain: bfloat16 [48], replicated, may hold values from 0.5 to 2
- gate_gain: bfloat16 [3072], P('fsdp'), may hold values from 0.5 to 1.5
- out_weight: bfloat16 [3072, 1536], P('fsdp'), may hold values from -0.109375 to 0.109375
Outputs:
- output: bfloat16 [8192, 1536], P(('rep', 'fsdp'))
- tokens_grad: bfloat16 [8192, 1536], P(('rep', 'fsdp'))
- grad_norm: float32 [1536], P('fsdp')
- grad_inproj: float32 [1536, 6448], P('fsdp')
- grad_kernel: float32 [4, 3328], P(None, 'fsdp')
- grad_convbias: float32 [3328], P('fsdp')
- grad_step: float32 [48], replicated
- grad_rate: float32 [48], replicated
- grad_skip: float32 [48], replicated
- grad_gate: float32 [3072], P('fsdp')
- grad_outproj: float32 [3072, 1536], P('fsdp')
Inputs may be any that keep to these rules, and one draw needn't show every extreme that they name: `segment_ids`: in each row the ids never fall; each of the 4 ids covers 1 to 128 consecutive slots, and some id covers exactly 128.
All inputs are finite; a program needn't handle non-finite values.
Results may differ from a plain program's by a relative error of at most 0.0072.
Values may be sent and summed in bfloat16 or wider, within the bound.
No kernel may reach another device: no remote copies, remote signals or barrier semaphores. Data moves between devices by JAX's collectives and lax.ppermute only.
A program may use at most 256 MiB of HBM per device.

v0:
```python
from functools import partial

import jax
import jax.numpy as jnp
from jax import lax
from jax.sharding import PartitionSpec as P

HEADS = 48
HEADDIM = 64
DSTATE = 128
KERNEL = 4
SPAN = 256
DI = 3072
CONV = 3328


HIGHEST = lax.Precision.HIGHEST
EPSILON = 1e-05


def prenorm(values, scaling):
    factor = lax.rsqrt(jnp.mean(values * values, axis=-1, keepdims=True) + EPSILON)
    return values * factor * scaling


def convolve(segments, conv_input, conv_kernel, conv_shift):
    token_count = conv_input.shape[0]
    padded = jnp.pad(conv_input, ((KERNEL - 1, 0), (0, 0)))
    padded_ids = jnp.concatenate([jnp.full((KERNEL - 1,), -1, jnp.int32), segments])
    summed = jnp.zeros_like(conv_input) + conv_shift
    for offset in range(KERNEL):
        matches = (padded_ids[offset : offset + token_count] == segments).astype(conv_input.dtype)
        summed = (
            summed + conv_kernel[offset] * padded[offset : offset + token_count] * matches[:, None]
        )
    return jax.nn.silu(summed)


def scan_blocks(segments, values_in, key_side, query_side, step_size, decay):
    token_count = values_in.shape[0]
    blocks = token_count // SPAN
    block_ids = segments.reshape(blocks, SPAN)
    before_ids = jnp.concatenate([jnp.full((1,), -1, jnp.int32), block_ids[:-1, -1]])
    places = jnp.arange(SPAN)
    lower = places[:, None] >= places[None, :]

    def advance(state, inputs):
        value_block, key_block, query_block, step_block, decay_block, id_block, prior = inputs
        running = jnp.cumsum(decay_block, axis=0)
        running_heads = running.T
        between = running_heads[:, :, None] - running_heads[:, None, :]
        allowed = lower & (id_block[:, None] == id_block[None, :])
        decays = jnp.where(allowed[None], jnp.exp(jnp.where(allowed[None], between, 0.0)), 0.0)
        affinity = jnp.dot(query_block, key_block.T, precision=HIGHEST)
        weights = decays * affinity[None] * step_block.T[:, None, :]
        local_part = jnp.einsum("hij,jhp->ihp", weights, value_block, precision=HIGHEST)
        reaching = (id_block == prior).astype(jnp.float32)[:, None] * jnp.exp(running)
        carried_part = (
            jnp.einsum("in,hpn->ihp", query_block, state, precision=HIGHEST) * reaching[:, :, None]
        )
        final_id = id_block[-1]
        keeping = (final_id == prior).astype(jnp.float32) * jnp.exp(running[-1])
        last_weight = (
            (id_block == final_id).astype(jnp.float32)[:, None]
            * jnp.exp(running[-1][None, :] - running)
            * step_block
        )
        fresh = jnp.einsum("jh,jhp,jn->hpn", last_weight, value_block, key_block, precision=HIGHEST)
        return (keeping[:, None, None] * state + fresh, local_part + carried_part)

    initial = jnp.zeros((HEADS, HEADDIM, DSTATE), jnp.float32)
    sliced = (
        values_in.reshape(blocks, SPAN, HEADS, HEADDIM),
        key_side.reshape(blocks, SPAN, DSTATE),
        query_side.reshape(blocks, SPAN, DSTATE),
        step_size.reshape(blocks, SPAN, HEADS),
        decay.reshape(blocks, SPAN, HEADS),
        block_ids,
        before_ids,
    )
    _, outputs = lax.scan(advance, initial, sliced)
    return outputs.reshape(token_count, HEADS, HEADDIM)


def mixer(
    segments, projected, conv_kernel, conv_shift, step_offset, rate_values, skip_weight, gate_scale
):
    token_count = projected.shape[0]
    gate_part = projected[:, :DI]
    conv_input = projected[:, DI : DI + CONV]
    step_input = projected[:, DI + CONV :]
    activated = convolve(segments, conv_input, conv_kernel, conv_shift)
    values_in = activated[:, :DI].reshape(token_count, HEADS, HEADDIM)
    key_side = activated[:, DI : DI + DSTATE]
    query_side = activated[:, DI + DSTATE :]
    step_size = jax.nn.softplus(step_input + step_offset)
    decay = -jnp.exp(rate_values) * step_size
    scanned = (
        scan_blocks(segments, values_in, key_side, query_side, step_size, decay)
        + skip_weight[None, :, None] * values_in
    )
    gated = scanned.reshape(token_count, DI) * jax.nn.silu(gate_part)
    factor = lax.rsqrt(jnp.mean(gated * gated, axis=-1, keepdims=True) + EPSILON)
    return gated * factor * gate_scale


def owner_order(values, position, groups, copies):
    shape = values.shape
    length = shape[position]
    viewed = values.reshape(
        shape[:position] + (groups, copies, length // (groups * copies)) + shape[position + 1 :]
    )
    return jnp.swapaxes(viewed, position, position + 1).reshape(shape)


def body(
    tokens,
    segment_ids,
    cotangent,
    norm_gain,
    in_weight,
    conv_weight,
    conv_bias,
    step_bias,
    rate_log,
    skip_gain,
    gate_gain,
    out_weight,
):
    groups = lax.axis_size("fsdp")
    copies = lax.axis_size("rep")
    segments = segment_ids[0]
    gathered = (
        lax.all_gather(norm_gain, "fsdp", axis=0, tiled=True),
        lax.all_gather(in_weight, "fsdp", axis=0, tiled=True),
        lax.all_gather(conv_weight, "fsdp", axis=1, tiled=True),
        lax.all_gather(conv_bias, "fsdp", axis=0, tiled=True),
        lax.all_gather(gate_gain, "fsdp", axis=0, tiled=True),
        lax.all_gather(out_weight, "fsdp", axis=0, tiled=True),
    )
    full_norm, full_in, full_kernel, full_shift, full_gate, full_out = gathered
    inputs32 = tokens.astype(jnp.float32)
    normed, norm_back = jax.vjp(prenorm, inputs32, full_norm.astype(jnp.float32))
    normed_low = normed.astype(jnp.bfloat16)
    projected = jnp.dot(normed_low, full_in, preferred_element_type=jnp.float32)
    mixed, mix_back = jax.vjp(
        partial(mixer, segments),
        projected,
        full_kernel.astype(jnp.float32),
        full_shift.astype(jnp.float32),
        step_bias.astype(jnp.float32),
        rate_log.astype(jnp.float32),
        skip_gain.astype(jnp.float32),
        full_gate.astype(jnp.float32),
    )
    mixed_low = mixed.astype(jnp.bfloat16)
    output = (inputs32 + jnp.dot(mixed_low, full_out, preferred_element_type=jnp.float32)).astype(
        jnp.bfloat16
    )
    back_in, back_out = (
        lax.all_gather(in_weight, "fsdp", axis=0, tiled=True),
        lax.all_gather(out_weight, "fsdp", axis=0, tiled=True),
    )
    grad_mixed = jnp.dot(cotangent, back_out.T, preferred_element_type=jnp.float32)
    grad_proj, grad_kernel, grad_shift, grad_step, grad_rate, grad_skip, grad_gate = mix_back(
        grad_mixed
    )
    grad_low = grad_proj.astype(jnp.bfloat16)
    grad_normed = jnp.dot(grad_low, back_in.T, preferred_element_type=jnp.float32)
    grad_through, grad_first = norm_back(grad_normed)
    tokens_grad = (cotangent.astype(jnp.float32) + grad_through).astype(jnp.bfloat16)
    contract = (((0,), (0,)), ((), ()))
    left_input = owner_order(normed_low, 1, groups, copies)
    left_output = owner_order(mixed_low, 1, groups, copies)
    small_terms = (
        owner_order(grad_first, 0, groups, copies),
        owner_order(grad_kernel, 1, groups, copies),
        owner_order(grad_shift, 0, groups, copies),
        owner_order(grad_gate, 0, groups, copies),
    )
    input_terms = lax.dot_general(
        left_input, grad_low, contract, preferred_element_type=jnp.float32
    )
    output_terms = lax.dot_general(
        left_output, cotangent, contract, preferred_element_type=jnp.float32
    )
    pieces = (
        small_terms[0],
        input_terms,
        small_terms[1],
        small_terms[2],
        small_terms[3],
        output_terms,
    )
    shares = (
        lax.psum_scatter(pieces[0], ("rep", "fsdp"), scatter_dimension=0, tiled=True),
        lax.psum_scatter(pieces[1], ("rep", "fsdp"), scatter_dimension=0, tiled=True),
        lax.psum_scatter(pieces[2], ("rep", "fsdp"), scatter_dimension=1, tiled=True),
        lax.psum_scatter(pieces[3], ("rep", "fsdp"), scatter_dimension=0, tiled=True),
        lax.psum_scatter(pieces[4], ("rep", "fsdp"), scatter_dimension=0, tiled=True),
        lax.psum_scatter(pieces[5], ("rep", "fsdp"), scatter_dimension=0, tiled=True),
    )
    totals = (
        lax.all_gather(shares[0], "rep", axis=0, tiled=True),
        lax.all_gather(shares[1], "rep", axis=0, tiled=True),
        lax.all_gather(shares[2], "rep", axis=1, tiled=True),
        lax.all_gather(shares[3], "rep", axis=0, tiled=True),
        lax.all_gather(shares[4], "rep", axis=0, tiled=True),
        lax.all_gather(shares[5], "rep", axis=0, tiled=True),
    )
    head_totals = lax.psum((grad_step, grad_rate, grad_skip), ("rep", "fsdp"))
    return (
        output,
        tokens_grad,
        totals[0],
        totals[1],
        totals[2],
        totals[3],
        head_totals[0],
        head_totals[1],
        head_totals[2],
        totals[4],
        totals[5],
    )


def solution(mesh):
    in_specs = (
        P(("rep", "fsdp"), None),
        P(("rep", "fsdp"), None),
        P(("rep", "fsdp"), None),
        P("fsdp"),
        P("fsdp", None),
        P(None, "fsdp"),
        P("fsdp"),
        P(),
        P(),
        P(),
        P("fsdp"),
        P("fsdp", None),
    )
    out_specs = (
        P(("rep", "fsdp"), None),
        P(("rep", "fsdp"), None),
        P("fsdp"),
        P("fsdp", None),
        P(None, "fsdp"),
        P("fsdp"),
        P(),
        P(),
        P(),
        P("fsdp"),
        P("fsdp", None),
    )
    return jax.shard_map(body, mesh=mesh, in_specs=in_specs, out_specs=out_specs, check_vma=False)
```

profile of v0, /device:TPU:0, one launch (start us, length us, event | category | flops | bytes accessed | tf_op | source)
XLA Modules:
  0.0 1203.1 jit_solution(6446954740561904133)
XLA Ops:
  8.1 0.7 all-gather.11.cloned.1.call-update
  8.8 9.6 all-gather
  18.5 8.2 all-gather.1
  28.9 9.8 all-reduce.18
  38.9 7.7 all-gather.2
  47.6 1.2 compare_convert_fusion
  48.8 0.7 fusion.54
  49.8 146.5 %all-gather.9.cloned.1.call-done = bf16[1536,6448]{0,1:T(8,128)(2,1)} async-done(((bf16[384,6448]{0,1:T(8,128)(2,1)}), bf16[1536,6448]{0,1:T(8,128)(2,1)}) %all-gather.9.cloned.1.call-update) | async-done | bytes 19808272 | tf_op jit(solution)/shard_map/all_gather | solution.py:135
  196.3 9.9 fusion.91
  206.6 7.5 fusion.23
  214.1 1.9 slice.115
  217.2 5.4 multiply_reduce_fusion.6
  222.7 1.7 fusion.81
  224.8 2.7 fusion.51
  227.5 16.2 %bitcast_add_fusion.3 = f32[256,48,64]{0,2,1:T(8,128)S(1)} fusion(f32[256,48,64]{0,2,1:T(8,128)S(1)} %fusion.51, f32[256,48,64]{0,2,1:T(8,128)S(1)} %bitcast.174, f32[48,256]{1,0:T(8,128)S(1)} %get-tuple-element.419, f32[256,256]{1,0:T(8,128)S(1)} %fusion.59, f32[48,256]{1,0:T(8,128)S(1)} %get-tuple-element.431, pred[256,256]{1,0:T(8,128)(4,1)S(1)} %copy-done.39, ...), kind=kOutput, calls=%fused_computation.51 | convolution fusion | flops 2433220608 | bytes 9912320 | tf_op jit(solution)/shard_map/jvp()/while/body/eval_jaxpr/hij,jhp->ihp/dot_general | solution.py:56
  243.8 5.3 multiply_reduce_fusion.11
  250.2 44.2 %all-gather.11.cloned.1.call-done = bf16[3072,1536]{1,0:T(8,128)(2,1)} async-done(((bf16[768,1536]{1,0:T(8,128)(2,1)}), bf16[3072,1536]{1,0:T(8,128)(2,1)}) %all-gather.11.cloned.1.call-update) | async-done | bytes 9437200 | tf_op jit(solution)/shard_map/all_gather | solution.py:139
  294.4 8.8 multiply_reduce_fusion.7
  303.3 7.1 multiply_reduce_fusion.8
  310.4 1.2 copy-done.8
  312.1 8.0 fusion.92
  320.1 2.3 copy.137
  322.4 2.1 copy.138
  324.5 0.7 copy.129
  325.2 4.1 multiply_reduce_fusion.9
  329.6 1.2 copy-done.5
  330.8 21.6 %fusion.8 = (f32[48,256]{1,0:T(8,128)S(1)}, f32[48,256]{1,0:T(8,128)S(1)}, f32[48,256]{1,0:T(8,128)}, f32[256,256]{1,0:T(8,128)}) fusion(f32[48,256]{1,0:T(8,128)} %copy-done.42, f32[256,256]{1,0:T(8,128)} %copy-done.22, f32[48,256]{1,0:T(8,128)S(1)} %copy-done.41, pred[256,256]{1,0:T(8,128)(4,1)} %fusion.54, f32[48,64,256]{2,1,0:T(8,128)S(1)} %bitcast.179, ...), kind=kOutput, calls=%fused_computation.10 | convolution fusion | flops 2463002624 | bytes 7127040 | tf_op jit(solution)/shard_map/transpose(jvp())/while/body/eval_jaxpr/hij,jhp->ihp/dot_general | solution.py:56
  352.5 1.6 copy_bitcast_fusion.1
  354.1 3.2 reduce-window.28
  358.0 1.3 reduce-window.29
  359.2 0.7 slice.105
  359.9 2.2 fusion.87
  362.1 13.7 %bitcast_add_fusion.1 = f32[256,48,64]{0,2,1:T(8,128)S(1)} fusion(f32[256,48,64]{0,2,1:T(8,128)} %get-tuple-element.438, f32[48,64,256]{2,1,0:T(8,128)} %bitcast.178, f32[48,256]{1,0:T(8,128)} %copy-done.42, f32[256,256]{1,0:T(8,128)} %copy-done.22, f32[48,256]{1,0:T(8,128)} %copy-done.40, pred[256,256]{1,0:T(8,128)(4,1)} %fusion.54, ...), kind=kOutput, calls=%fused_computation.48 | convolution fusion | flops 2433220608 | bytes 9912320 | tf_op jit(solution)/shard_map/transpose(jvp())/while/body/eval_jaxpr/hij,jhp->ihp/dot_general | solution.py:56
  375.8 2.3 bitcast_multiply_fusion
  378.1 1.8 convolution_bitcast_fusion
  380.0 2.0 fusion.44
  382.8 8.7 multiply_reduce_fusion.4
  391.5 2.4 broadcast_multiply_fusion
  394.0 2.7 pad_add_fusion
  396.7 18.3 %fusion.84 = f32[1536,6448]{1,0:T(8,128)} fusion(bf16[256,1536]{0,1:T(8,128)(2,1)} %bitcast.184, f32[256,3072]{0,1:T(8,128)S(1)} %copy-done.13, f32[256,3328]{0,1:T(8,128)S(1)} %pad_add_fusion, f32[256,48]{0,1:T(8,128)S(1)} %copy-done.25), kind=kOutput, calls=%fused_computation.168 | convolution fusion | flops 5075865600 | bytes 47005696 | tf_op jit(solution)/shard_map/dot_general | solution.py:181
  415.7 14.8 %fusion.37 = (f32[1536]{0:T(1024)}, f32[256]{0:T(256)}, f32[256,1536]{1,0:T(8,128)}) fusion(bf16[256,1536]{1,0:T(8,128)(2,1)} %param.12, f32[256]{0:T(256)S(1)} %copy-done.57, f32[1536]{0:T(1024)S(1)} %copy-done.38, bf16[1536,6448]{0,1:T(8,128)(2,1)} %all-gather.9.cloned.1.call-done, f32[256,3072]{0,1:T(8,128)} %get-tuple-element.415, ...), kind=kOutput, calls=%fused_computation.74 | convolution fusion | flops 5078616064 | bytes 28784640 | tf_op jit(solution)/shard_map/dot_general | solution.py:169
  430.5 0.9 reshape.447
  432.3 0.8 reshape.456
  433.2 0.7 reshape.458
  433.9 0.8 reduce_sum.259
  435.3 0.8 reshape.459
  436.8 1.2 negate_multiply_fusion
  438.0 89.1 %reduce-scatter.6.cloned.1.call-done = f32[96,1536]{1,0:T(8,128)} async-done(((f32[3072,1536]{1,0:T(8,128)}), f32[96,1536]{1,0:T(8,128)}) %reduce-scatter.6.cloned.1.call-update) | async-done | bytes 589840 | tf_op jit(solution)/shard_map/reduce_scatter | solution.py:201
  527.2 369.0 %reduce-scatter.4.cloned.1.call-done = f32[48,6448]{1,0:T(8,128)} async-done(((f32[1536,6448]{1,0:T(8,128)}), f32[48,6448]{1,0:T(8,128)}) %reduce-scatter.4.cloned.1.call-update) | async-done | bytes 1238032 | tf_op jit(solution)/shard_map/reduce_scatter | solution.py:197
  896.2 1.2 dynamic-slice.4
  899.4 0.7 multiply_multiply_fusion.5
  900.1 2.8 fusion.39
  902.9 7.2 fusion.29
  910.1 118.4 %all-reduce.30.cloned.1.call-done = (f32[1536]{0:T(1024)}, f32[4,3328]{1,0:T(4,128)}, f32[3328]{0:T(1024)}, f32[48]{0:T(128)}, f32[48]{0:T(128)}, /*index=5*/f32[48]{0:T(128)}, f32[3072]{0:T(1024)}) async-done(((f32[1536]{0:T(1024)}, f32[4,3328]{1,0:T(4,128)}, f32[3328]{0:T(1024)}, f32[48]{0:T(128)}, f32[48]{0:T(128)}, /*index=5*/f32[48]{0:T(128)}, f32[3072]{0:T(1024)}), (f32[1536]{0:T(1024)}, ...) | async-done | bytes 85584
  1028.5 0.8 dynamic-slice_bitcast_fusion
  1029.3 13.7 %all-gather.3 = f32[8,104,4]{1,2,0:T(4,128)S(1)} all-gather(f32[1,104,4]{1,2,0:T(4,128)S(1)} %dynamic-slice_bitcast_fusion), channel_id=1, replica_groups=mesh['rep'=8,'fsdp'=4] {'rep'}, dimensions={0}, use_global_device_ids=true | all-gather | bytes 14976 | tf_op jit(solution)/shard_map/all_gather | solution.py:206
  1043.6 0.9 dynamic-slice_dynamic-update-slice_fusion.1
  1044.5 0.9 dynamic-slice_dynamic-update-slice_fusion.2
  1045.3 0.9 dynamic-slice_dynamic-update-slice_fusion
  1046.2 30.1 %all-reduce.27 = (f32[384]{0:T(512)}, f32[832]{0:T(1024)}, f32[768]{0:T(1024)}) all-reduce(f32[384]{0:T(512)S(1)} %dynamic-slice_dynamic-update-slice_fusion.2, f32[832]{0:T(1024)S(1)} %dynamic-slice_dynamic-update-slice_fusion.1, f32[768]{0:T(1024)S(1)} %dynamic-slice_dynamic-update-slice_fusion), channel_id=1, replica_groups=mesh['rep'=8,'fsdp'=4] {'rep'}, use_global_device_ids=true, to_apply=%add.19 | all-reduce | flops 1984 | bytes 15872
  1076.3 6.5 all-gather.15.cloned.1.call-done
  1082.8 96.0 %all-gather.13.cloned.1.call-done = f32[384,6448]{1,0:T(8,128)} async-done(((f32[48,6448]{1,0:T(8,128)}), f32[384,6448]{1,0:T(8,128)}) %all-gather.13.cloned.1.call-update) | async-done | bytes 9904144 | tf_op jit(solution)/shard_map/all_gather | solution.py:205
  1178.8 10.7 copy.145
  1191.0 4.8 copy.202
  (226 shorter events, 14.5 us)
Async XLA Ops:
  7.2 20.2 %copy-start.78 = (u32[32]{0:T(128)S(1)}, u32[32]{0:T(128)}, u32[]{:S(2)}) copy-start(u32[32]{0:T(128)} %constant.209) | copy-start | bytes 388
  7.2 11.3 copy-start.65
  7.2 19.6 %copy-start.55 = (s32[1,256]{1,0:T(1,128)S(1)}, s32[1,256]{1,0:T(1,128)}, u32[]{:S(2)}) copy-start(s32[1,256]{1,0:T(1,128)} %param.13) | copy-start | bytes 3076
  7.2 21.4 %copy-start.69 = (bf16[832]{0:T(1024)(128)(2,1)S(1)}, bf16[832]{0:T(1024)(128)(2,1)}, u32[]{:S(2)}) copy-start(bf16[832]{0:T(1024)(128)(2,1)} %param.18) | copy-start | bytes 4996
  7.2 31.5 %copy-start.72 = (bf16[48]{0:T(256)(128)(2,1)S(1)}, bf16[48]{0:T(256)(128)(2,1)}, u32[]{:S(2)}) copy-start(bf16[48]{0:T(256)(128)(2,1)} %param.21) | copy-start | bytes 292
  7.2 31.6 %copy-start.73 = (bf16[48]{0:T(256)(128)(2,1)S(1)}, bf16[48]{0:T(256)(128)(2,1)}, u32[]{:S(2)}) copy-start(bf16[48]{0:T(256)(128)(2,1)} %param.19) | copy-start | bytes 292
  7.3 31.6 %copy-start.70 = (bf16[768]{0:T(1024)(128)(2,1)S(1)}, bf16[768]{0:T(1024)(128)(2,1)}, u32[]{:S(2)}) copy-start(bf16[768]{0:T(1024)(128)(2,1)} %param.22) | copy-start | bytes 4612
  7.3 39.5 %copy-start.11 = (bf16[256,1536]{1,0:T(8,128)(2,1)S(1)}, bf16[256,1536]{1,0:T(8,128)(2,1)}, u32[]{:S(2)}) copy-start(bf16[256,1536]{1,0:T(8,128)(2,1)} %param.12) | copy-start | bytes 2359300
  7.3 39.8 %copy-start.74 = (bf16[48]{0:T(256)(128)(2,1)S(1)}, bf16[48]{0:T(256)(128)(2,1)}, u32[]{:S(2)}) copy-start(bf16[48]{0:T(256)(128)(2,1)} %param.20) | copy-start | bytes 292
  7.3 189.1 %all-gather.9.cloned.1.call-start = ((), (), s32[]{:S(2)}) async-start(), calls=%async_computation.2 | async-start | bytes 24760320 | tf_op jit(solution)/shard_map/all_gather | solution.py:135
  8.0 286.4 %all-gather.11.cloned.1.call-start = ((), (), s32[]{:S(2)}) async-start(), calls=%async_computation.3 | async-start | bytes 11796480 | tf_op jit(solution)/shard_map/all_gather | solution.py:139
  8.8 518.3 %reduce-scatter.6.cloned.1.call-start = ((), (), s32[]{:S(2)}) async-start(), calls=%async_computation.6 | async-start | bytes 19464192 | tf_op jit(solution)/shard_map/reduce_scatter | solution.py:201
  18.5 187.8 %copy-start.37 = (f32[1536]{0:T(1024)}, f32[1536]{0:T(1024)S(1)}, u32[]{:S(2)}) copy-start(f32[1536]{0:T(1024)S(1)} %reshape.483) | copy-start | bytes 18436
  38.9 264.4 %copy-start.26 = (f32[3072]{0:T(1024)}, f32[3072]{0:T(1024)S(1)}, u32[]{:S(2)}) copy-start(f32[3072]{0:T(1024)S(1)} %mul.627) | copy-start | bytes 36868
  38.9 177.1 %copy-start.60 = (f32[48]{0:T(128)}, f32[48]{0:T(128)S(1)}, u32[]{:S(2)}) copy-start(f32[48]{0:T(128)S(1)} %convert_element_type.102) | copy-start | bytes 580
  46.8 159.8 %copy-start.28 = (f32[3328]{0:T(1024)}, f32[3328]{0:T(1024)S(1)}, u32[]{:S(2)}) copy-start(f32[3328]{0:T(1024)S(1)} %get-tuple-element.392) | copy-start | bytes 39940
  46.8 159.8 %copy-start.30 = (f32[3328]{0:T(1024)}, f32[3328]{0:T(1024)S(1)}, u32[]{:S(2)}) copy-start(f32[3328]{0:T(1024)S(1)} %get-tuple-element.393) | copy-start | bytes 39940
  46.8 159.8 %copy-start.32 = (f32[3328]{0:T(1024)}, f32[3328]{0:T(1024)S(1)}, u32[]{:S(2)}) copy-start(f32[3328]{0:T(1024)S(1)} %get-tuple-element.394) | copy-start | bytes 39940
  46.8 159.8 %copy-start.34 = (f32[3328]{0:T(1024)}, f32[3328]{0:T(1024)S(1)}, u32[]{:S(2)}) copy-start(f32[3328]{0:T(1024)S(1)} %get-tuple-element.395) | copy-start | bytes 39940
  47.1 168.9 %copy-start.67 = (f32[48]{0:T(128)}, f32[48]{0:T(128)S(1)}, u32[]{:S(2)}) copy-start(f32[48]{0:T(128)S(1)} %fusion.74) | copy-start | bytes 580
  47.1 159.2 %copy-start.56 = (f32[256]{0:T(256)}, f32[256]{0:T(256)S(1)}, u32[]{:S(2)}) copy-start(f32[256]{0:T(256)S(1)} %fusion.72) | copy-start | bytes 3076
  48.8 157.8 %copy-start.45 = (f32[256]{0:T(256)}, f32[256]{0:T(256)S(1)}, u32[]{:S(2)}) copy-start(f32[256]{0:T(256)S(1)} %get-tuple-element.433) | copy-start | bytes 3076
  48.8 157.8 %copy-start.47 = (f32[256]{0:T(256)}, f32[256]{0:T(256)S(1)}, u32[]{:S(2)}) copy-start(f32[256]{0:T(256)S(1)} %get-tuple-element.434) | copy-start | bytes 3076
  48.8 157.8 %copy-start.49 = (f32[256]{0:T(256)}, f32[256]{0:T(256)S(1)}, u32[]{:S(2)}) copy-start(f32[256]{0:T(256)S(1)} %get-tuple-element.435) | copy-start | bytes 3076
  49.8 156.5 %copy-start.18 = (bf16[256,1536]{1,0:T(8,128)(2,1)}, bf16[256,1536]{1,0:T(8,128)(2,1)S(1)}, u32[]{:S(2)}) copy-start(bf16[256,1536]{1,0:T(8,128)(2,1)S(1)} %fusion.36) | copy-start | bytes 2359300
  206.3 9.7 copy-start.7
  206.5 7.6 copy-start
  216.9 5.8 copy-start.61
  216.9 7.4 copy-start.43
  217.0 10.5 copy-start.40
  217.2 7.2 copy-start.63
  224.4 19.3 %copy-start.23 = (f32[256,48]{0,1:T(8,128)}, f32[256,48]{0,1:T(8,128)S(1)}, u32[]{:S(2)}) copy-start(f32[256,48]{0,1:T(8,128)S(1)} %get-tuple-element.427) | copy-start | bytes 147460
  224.4 19.4 %copy-start.42 = (f32[48,256]{1,0:T(8,128)}, f32[48,256]{1,0:T(8,128)S(1)}, u32[]{:S(2)}) copy-start(f32[48,256]{1,0:T(8,128)S(1)} %get-tuple-element.419) | copy-start | bytes 147460
  224.8 18.9 %copy-start.22 = (f32[256,256]{1,0:T(8,128)}, f32[256,256]{1,0:T(8,128)S(1)}, u32[]{:S(2)}) copy-start(f32[256,256]{1,0:T(8,128)S(1)} %fusion.59) | copy-start | bytes 786436
  227.5 16.2 %copy-start.14 = (f32[256,48,64]{0,2,1:T(8,128)}, f32[256,48,64]{0,2,1:T(8,128)S(1)}, u32[]{:S(2)}) copy-start(f32[256,48,64]{0,2,1:T(8,128)S(1)} %fusion.51) | copy-start | bytes 9437188
  294.4 8.8 copy-start.59
  294.4 8.8 copy-start.16
  294.4 8.8 copy-start.17
  294.4 8.9 copy-start.66
  320.1 576.1 %reduce-scatter.4.cloned.1.call-start = ((), (), s32[]{:S(2)}) async-start(), calls=%async_computation.4 | async-start | bytes 41361408 | tf_op jit(solution)/shard_map/reduce_scatter | solution.py:197
  330.8 21.7 %copy-start.36 = (f32[1,48]{0,1:T(8,128)S(1)}, f32[1,48]{0,1:T(8,128)}, u32[]{:S(2)}) copy-start(f32[1,48]{0,1:T(8,128)} %copy.129) | copy-start | bytes 580
  330.8 21.7 %copy-start.44 = (f32[48,2]{0,1:T(2,128)S(1)}, f32[48,2]{0,1:T(2,128)}, u32[]{:S(2)}) copy-start(f32[48,2]{0,1:T(2,128)} %copy-done.43) | copy-start | bytes 1156
  330.8 21.7 %copy-start.51 = (f32[256]{0:T(256)S(1)}, f32[256]{0:T(256)}, u32[]{:S(2)}) copy-start(f32[256]{0:T(256)} %get-tuple-element.432) | copy-start | bytes 3076
  330.8 21.7 %copy-start.52 = (f32[256]{0:T(256)S(1)}, f32[256]{0:T(256)}, u32[]{:S(2)}) copy-start(f32[256]{0:T(256)} %get-tuple-element.436) | copy-start | bytes 3076
  330.8 21.7 %copy-start.62 = (f32[48]{0:T(128)S(1)}, f32[48]{0:T(128)}, u32[]{:S(2)}) copy-start(f32[48]{0:T(128)} %copy-done.60) | copy-start | bytes 580
  330.8 21.7 %copy-start.64 = (f32[48]{0:T(128)S(1)}, f32[48]{0:T(128)}, u32[]{:S(2)}) copy-start(f32[48]{0:T(128)} %copy-done.63) | copy-start | bytes 580
  362.1 13.7 %copy-start.6 = (f32[256,3072]{0,1:T(8,128)S(1)}, f32[256,3072]{0,1:T(8,128)}, u32[]{:S(2)}) copy-start(f32[256,3072]{0,1:T(8,128)} %get-tuple-element.407) | copy-start | bytes 9437188
  362.1 13.7 %copy-start.24 = (f32[256,48]{0,1:T(8,128)S(1)}, f32[256,48]{0,1:T(8,128)}, u32[]{:S(2)}) copy-start(f32[256,48]{0,1:T(8,128)} %copy-done.23) | copy-start | bytes 147460
  362.1 13.7 %copy-start.27 = (f32[3072]{0:T(1024)S(1)}, f32[3072]{0:T(1024)}, u32[]{:S(2)}) copy-start(f32[3072]{0:T(1024)} %copy-done.26) | copy-start | bytes 36868
  375.8 6.9 copy-start.10
  382.7 8.7 copy-start.29
  382.8 8.7 copy-start.31
  382.8 8.7 copy-start.33
  382.8 8.7 copy-start.35
  415.0 484.4 %copy-start.54 = (f32[256]{0:T(256)S(1)}, f32[256]{0:T(256)}, u32[]{:S(2)}) copy-start(f32[256]{0:T(256)} %copy-done.53) | copy-start | bytes 3076
  415.0 613.5 %all-reduce.30.cloned.1.call-start = ((), (), s32[]{:S(2)}) async-start(), calls=%async_computation.8 | async-start | bytes 183296
  430.5 469.6 %copy-start.12 = (bf16[256,1536]{1,0:T(8,128)(2,1)S(1)}, bf16[256,1536]{1,0:T(8,128)(2,1)}, u32[]{:S(2)}) copy-start(bf16[256,1536]{1,0:T(8,128)(2,1)} %param.12) | copy-start | bytes 2359300
  430.5 469.6 %copy-start.20 = (bf16[256,1536]{1,0:T(8,128)(2,1)S(1)}, bf16[256,1536]{1,0:T(8,128)(2,1)}, u32[]{:S(2)}) copy-start(bf16[256,1536]{1,0:T(8,128)(2,1)} %param.14) | copy-start | bytes 2359300
  432.1 470.8 %copy-start.9 = (bf16[256,3072]{0,1:T(8,128)(2,1)S(1)}, bf16[256,3072]{0,1:T(8,128)(2,1)}, u32[]{:S(2)}) copy-start(bf16[256,3072]{0,1:T(8,128)(2,1)} %copy-done.8) | copy-start | bytes 4718596
  438.0 644.8 %all-gather.15.cloned.1.call-start = ((), (), s32[]{:S(2)}) async-start(), calls=%async_computation.7 | async-start | bytes 5308416 | tf_op jit(solution)/shard_map/all_gather | solution.py:209
  527.1 651.6 %all-gather.13.cloned.1.call-start = ((), (), s32[]{:S(2)}) async-start(), calls=%async_computation.5 | async-start | bytes 11280384 | tf_op jit(solution)/shard_map/all_gather | solution.py:205
  1076.3 113.1 %copy-start.77 = (f32[48]{0:T(128)S(1)}, f32[48]{0:T(128)}, u32[]{:S(2)}) copy-start(f32[48]{0:T(128)} %get-tuple-element.458) | copy-start | bytes 580
  1076.3 113.7 %copy-start.76 = (f32[48]{0:T(128)S(1)}, f32[48]{0:T(128)}, u32[]{:S(2)}) copy-start(f32[48]{0:T(128)} %get-tuple-element.459) | copy-start | bytes 580
  1076.3 114.2 %copy-start.75 = (f32[48]{0:T(128)S(1)}, f32[48]{0:T(128)}, u32[]{:S(2)}) copy-start(f32[48]{0:T(128)} %get-tuple-element.460) | copy-start | bytes 580
  (22 other events, 71.7 us)
Sparse Core Ops, SparseCore 0:
  9.9 186.3 all-gather.8
  198.2 96.1 all-gather.10
  320.2 206.8 reduce-scatter.5
  533.4 362.7 reduce-scatter.3
  903.6 124.8 all-reduce.29
  1030.0 52.7 all-gather.14
  1084.4 94.2 all-gather.12
where the time goes:
time: 1210 us; the launch traced here: 1200 us
  waiting for transfers between devices  871 us (72%)
  matrix products  131 us (11%)
  blocking collectives  79.1 us (7%)
  other arithmetic  59.4 us (5%)
  local copies, waits for them, and re-layouts  43.5 us (4%)
  between operations  18.3 us (2%)
    reduce_scatter x1, waiting for transfers between devices, body(): lax.psum_scatter(pieces[1], ('rep', 'fsdp'), scatter_dimension=0, tiled=T...  369 us
    all_gather x1, waiting for transfers between devices, body(): lax.all_gather(in_weight, 'fsdp', axis=0, tiled=True)  147 us
    unnamed x8, waiting for transfers between devices  120 us
    all_gather x1, waiting for transfers between devices, body(): lax.all_gather(shares[1], 'rep', axis=0, tiled=True)  96 us
    reduce_scatter x1, waiting for transfers between devices, body(): lax.psum_scatter(pieces[5], ('rep', 'fsdp'), scatter_dimension=0, tiled=T...  89.1 us
    dot_general x3, matrix products, advance(): jnp.einsum('hij,jhp->ihp', weights, value_block, precision=HIGHEST)  51.5 us
    all_gather x1, waiting for transfers between devices, body(): lax.all_gather(out_weight, 'fsdp', axis=0, tiled=True)  44.2 us
    unnamed x2, blocking collectives  40 us
  transfers between devices with their start and end apart: 7, of which 7 were waited for; matrix products, arithmetic and copies ran while one was open for 16% of the time, Pallas kernels for 0%

commit v1 on v0

v1 whole, which is shorter than its diff:
```python
from functools import partial

import jax
import jax.numpy as jnp
from jax import lax
from jax.experimental import pallas as pl
from jax.experimental.pallas import tpu as pltpu
from jax.sharding import PartitionSpec as P

HEADS = 48
HEADDIM = 64
DSTATE = 128
KERNEL = 4
LANES = 128
EPSILON = 1e-05
BF = jnp.bfloat16
F32 = jnp.float32
HIGHEST = lax.Precision.HIGHEST
VMEM_LIMIT = 60 * 1024 * 1024

NN = (((1,), (0,)), ((), ()))
NT = (((1,), (1,)), ((), ()))
TN = (((0,), (0,)), ((), ()))


def mm(a, b, dims):
    return lax.dot_general(a, b, dims, preferred_element_type=F32)


def mm_full(a, b, dims):
    return lax.dot_general(a, b, dims, precision=HIGHEST, preferred_element_type=F32)


def silu_parts(v):
    gate = jax.nn.sigmoid(v)
    return v * gate, gate * (1.0 + v * (1.0 - gate))


def call(kernel, out_shape, flops, moved, **kw):
    return pl.pallas_call(
        kernel,
        out_shape=out_shape,
        cost_estimate=pl.CostEstimate(flops=flops, bytes_accessed=moved, transcendentals=0),
        compiler_params=pltpu.CompilerParams(vmem_limit_bytes=VMEM_LIMIT),
        **kw,
    )


VM = pl.BlockSpec(memory_space=pltpu.VMEM)
HBM = pl.BlockSpec(memory_space=pl.ANY)


def inproj_kernel(groups, *refs):
    tokens = refs[:groups]
    gain_ref = refs[groups]
    place_ref = refs[groups + 1]
    own_ref = refs[groups + 2]
    near = refs[groups + 3 : 2 * groups + 2]
    far = refs[2 * groups + 2 : 3 * groups + 1]
    normed_ref, proj_ref, weight_ref, sems = refs[3 * groups + 1 :]
    member, core = place_ref[0], place_ref[1]
    rows = own_ref.shape[0]
    half = rows // 2
    copies = [
        pltpu.make_async_copy(
            own_ref, weight_ref.at[pl.ds(pl.multiple_of(member * rows, 16), rows), :], sems.at[0]
        )
    ]
    for k in range(1, groups):
        base = jnp.bitwise_xor(member, k) * rows
        first = pl.multiple_of(base + core * half, 16)
        second = pl.multiple_of(base + (1 - core) * half, 16)
        copies.append(
            pltpu.make_async_copy(near[k - 1], weight_ref.at[pl.ds(first, half), :], sems.at[2 * k - 1])
        )
        copies.append(
            pltpu.make_async_copy(far[k - 1], weight_ref.at[pl.ds(second, half), :], sems.at[2 * k])
        )
    for copy in copies:
        copy.start()
    span = tokens[0].shape[0]
    gain = gain_ref[...]
    for r in range(groups):
        x = tokens[r][...].astype(F32)
        factor = lax.rsqrt(jnp.mean(x * x, axis=-1, keepdims=True) + EPSILON)
        normed_ref[r * span : (r + 1) * span, :] = (x * factor * gain).astype(BF)
    for copy in copies:
        copy.wait()
    width = 384
    total = weight_ref.shape[1] // width

    def column(n, carry):
        at = pl.multiple_of(n * width, LANES)
        for r in range(groups):
            proj_ref[r * span : (r + 1) * span, pl.ds(at, width)] = mm(
                normed_ref[r * span : (r + 1) * span, :], weight_ref[:, pl.ds(at, width)], NN
            )
        return carry

    lax.fori_loop(0, total, column, 0)


def conv_forward(x, masks, taps, shift):
    total = shift + taps[KERNEL - 1] * x
    for s in range(1, KERNEL):
        total = total + taps[KERNEL - 1 - s] * (pltpu.roll(x, s, 0) * masks[s - 1])
    return total


def conv_backward(grad, x, masks, taps):
    span = x.shape[0]
    back = taps[KERNEL - 1] * grad
    tap_grads = [None] * KERNEL
    tap_grads[KERNEL - 1] = jnp.sum(grad * x, axis=0, keepdims=True)
    for s in range(1, KERNEL):
        part = grad * masks[s - 1]
        back = back + taps[KERNEL - 1 - s] * pltpu.roll(part, span - s, 0)
        tap_grads[KERNEL - 1 - s] = jnp.sum(part * pltpu.roll(x, s, 0), axis=0, keepdims=True)
    return back, tap_grads


def wide(column, count):
    return jnp.concatenate([column] * (count // LANES), axis=1)


def segment_masks(seg_ref):
    span = seg_ref.shape[-1]
    row = seg_ref[0:1, :]
    column = jnp.broadcast_to(row, (LANES, span)).T
    token = lax.broadcasted_iota(jnp.int32, (span, LANES), 0)
    masks = []
    for s in range(1, KERNEL):
        same = (pltpu.roll(column, s, 0) == column) & (token >= s)
        masks.append(jnp.where(same, 1.0, 0.0))
    i = lax.broadcasted_iota(jnp.int32, (span, span), 0)
    j = lax.broadcasted_iota(jnp.int32, (span, span), 1)
    allowed = (i >= j) & (wide(column, span) == row)
    lower = jnp.where(i >= j, 1.0, 0.0)
    return masks, jnp.where(allowed, 1.0, 0.0), lower


def row_setup(shared_ref, seg_ref, taps_ref, head_ref, member, per, saved):
    (mask_ref, affinity_ref, step_ref, run_ref, runt_ref, extra) = saved
    masks, allowed, lower = segment_masks(seg_ref)
    for s in range(KERNEL - 1):
        mask_ref[s] = masks[s]
    outs = []
    for c in range(2):
        at = slice(c * LANES, (c + 1) * LANES)
        taps = [taps_ref[k : k + 1, at] for k in range(KERNEL)]
        total = conv_forward(shared_ref[:, at], masks, taps, taps_ref[KERNEL : KERNEL + 1, at])
        outs.append((total, silu_parts(total)))
    keys, queries = outs[0][1][0], outs[1][1][0]
    affinity_ref[...] = mm_full(queries, keys, NT) * allowed
    raw = pltpu.roll(shared_ref[:, 2 * LANES :], lax.rem(LANES - member * per, LANES), 1)
    raw = raw + head_ref[0:1, :]
    step = jnp.maximum(raw, 0.0) + jnp.log1p(jnp.exp(-jnp.abs(raw)))
    run = mm_full(lower, -head_ref[1:2, :] * step, NN)
    step_ref[...] = step
    run_ref[...] = run
    runt_ref[...] = run.T
    if extra is not None:
        allowed_ref, lower_ref, raw_ref, sum_ref, keys_ref, queries_ref = extra
        allowed_ref[...] = allowed
        lower_ref[...] = lower
        raw_ref[...] = raw
        sum_ref[:, :LANES] = outs[0][0]
        sum_ref[:, LANES:] = outs[1][0]
        keys_ref[...] = keys
        queries_ref[...] = queries


def pair_decays(pair, run_ref, runt_ref, step_ref):
    back = lax.rem(LANES - 2 * pair, LANES)
    runs = pltpu.roll(run_ref[...], back, 1)
    steps = pltpu.roll(step_ref[...], back, 1)
    span = runs.shape[0]
    lane = lax.broadcasted_iota(jnp.int32, (span, LANES), 1)
    low = lane < HEADDIM
    stepx = jnp.where(low, steps[:, 0:1], steps[:, 1:2])
    decays = []
    for e in range(2):
        row = runt_ref[pl.ds(2 * pair + e, 1), :]
        decays.append(jnp.exp(jnp.minimum(runs[:, e : e + 1] - row, 0.0)))
    return decays, stepx, steps, low, lane


def forward_kernel(
    per,
    place_ref,
    z_ref,
    v_ref,
    shared_ref,
    seg_ref,
    taps_s_ref,
    taps_v_ref,
    head_ref,
    scanned_ref,
    gated_ref,
    square_ref,
    mask_ref,
    affinity_ref,
    step_ref,
    run_ref,
    runt_ref,
    total_ref,
):
    pair = pl.program_id(1)
    saved = (mask_ref, affinity_ref, step_ref, run_ref, runt_ref, None)

    @pl.when(pair == 0)
    def _():
        row_setup(shared_ref, seg_ref, taps_s_ref, head_ref, place_ref[0], per, saved)
        total_ref[...] = jnp.zeros_like(total_ref)

    masks = [mask_ref[s] for s in range(KERNEL - 1)]
    taps = [taps_v_ref[k : k + 1, :] for k in range(KERNEL)]
    values = silu_parts(conv_forward(v_ref[...], masks, taps, taps_v_ref[KERNEL : KERNEL + 1, :]))[0]
    decays, stepx, _, low, _ = pair_decays(pair, run_ref, runt_ref, step_ref)
    affinity = affinity_ref[...]
    fed = (stepx * values).astype(BF)
    first = mm((decays[0] * affinity).astype(BF), fed, NN)
    second = mm((decays[1] * affinity).astype(BF), fed, NN)
    inner = jnp.where(low, first, second)
    scanned = inner + taps_v_ref[KERNEL + 1 : KERNEL + 2, :] * values
    z = z_ref[...]
    g = scanned * (z * jax.nn.sigmoid(z))
    scanned_ref[...] = scanned
    gated_ref[...] = (g * taps_v_ref[KERNEL + 2 : KERNEL + 3, :]).astype(BF)
    total_ref[...] = total_ref[...] + g * g

    @pl.when(pair == pl.num_programs(1) - 1)
    def _():
        row = jnp.sum(total_ref[...].T, axis=0, keepdims=True)
        square_ref[...] = jnp.broadcast_to(row, square_ref.shape)


def mixgrad_kernel(groups, *refs):
    cots = refs[:groups]
    out_w_ref, gated_ref, square_ref, dm_ref, sums_ref = refs[groups:]
    span = cots[0].shape[0]
    weight = out_w_ref[...]
    for r in range(groups):
        at = slice(r * span, (r + 1) * span)
        dm = mm(cots[r][...], weight, NT)
        dm_ref[at, :] = dm
        prod = dm * gated_ref[at, :].astype(F32)
        part = prod[:, :LANES]
        for c in range(1, prod.shape[1] // LANES):
            part = part + prod[:, c * LANES : (c + 1) * LANES]
        row = jnp.sum(part.T, axis=0, keepdims=True)
        sub = lax.broadcasted_iota(jnp.int32, (8, span), 0)
        sums_ref[8 * r : 8 * r + 8, :] = jnp.where(sub == 0, square_ref[8 * r : 8 * r + 8, :], row)


def outproj_kernel(groups, gated_ref, out_w_ref, *outs):
    span = outs[0].shape[0]
    weight = out_w_ref[...]
    for r in range(groups):
        outs[r][...] = mm(gated_ref[r * span : (r + 1) * span, :], weight, NN).astype(outs[r].dtype)


def gate_scales(parts, width):
    total = parts[0]
    for part in parts[1:]:
        total = total + part
    square, cross = total[0:1, :], total[1:2, :]
    factor = lax.rsqrt(square / width + EPSILON)
    bend = factor * factor * factor * (cross / width)
    span = total.shape[1]
    return (
        jnp.broadcast_to(factor, (LANES, span)).T,
        jnp.broadcast_to(bend, (LANES, span)).T,
    )


def gatebwd_kernel(groups, width, *refs):
    sums = refs[:groups]
    z_ref, scanned_ref, dm_ref, gain_ref, gz_ref, ds_ref, mixed_ref, gate_ref = refs[groups:]
    r = pl.program_id(0)
    factor, bend = gate_scales([s[...] for s in sums], width)

    @pl.when(r == 0)
    def _():
        gate_ref[...] = jnp.zeros_like(gate_ref)

    for c in range(z_ref.shape[1] // LANES):
        at = slice(c * LANES, (c + 1) * LANES)
        gain = gain_ref[0:1, at]
        sz, dsz = silu_parts(z_ref[:, at])
        scanned = scanned_ref[:, at]
        dm = dm_ref[:, at]
        g = scanned * sz
        scaled = g * factor
        dg = factor * (dm * gain) - g * bend
        mixed_ref[:, at] = (scaled * gain).astype(BF)
        gz_ref[:, at] = (dg * scanned * dsz).astype(BF)
        ds_ref[:, at] = dg * sz
        gate_ref[0:1, at] += jnp.sum(dm * scaled, axis=0, keepdims=True)


def backward_kernel(
    per,
    place_ref,
    ds_ref,
    v_ref,
    scanned_ref,
    shared_ref,
    seg_ref,
    taps_s_ref,
    taps_v_ref,
    head_ref,
    gv_ref,
    gs_ref,
    vsum_ref,
    ssum_ref,
    mask_ref,
    affinity_ref,
    step_ref,
    run_ref,
    runt_ref,
    allowed_ref,
    lower_ref,
    raw_ref,
    sum_ref,
    keys_ref,
    queries_ref,
    daff_ref,
    dstep_ref,
    drun_ref,
):
    row, pair = pl.program_id(0), pl.program_id(1)
    extra = (allowed_ref, lower_ref, raw_ref, sum_ref, keys_ref, queries_ref)
    saved = (mask_ref, affinity_ref, step_ref, run_ref, runt_ref, extra)

    @pl.when((row == 0) & (pair == 0))
    def _():
        vsum_ref[...] = jnp.zeros_like(vsum_ref)
        ssum_ref[...] = jnp.zeros_like(ssum_ref)

    @pl.when(pair == 0)
    def _():
        row_setup(shared_ref, seg_ref, taps_s_ref, head_ref, place_ref[0], per, saved)
        daff_ref[...] = jnp.zeros_like(daff_ref)
        dstep_ref[...] = jnp.zeros_like(dstep_ref)
        drun_ref[...] = jnp.zeros_like(drun_ref)

    masks = [mask_ref[s] for s in range(KERNEL - 1)]
    taps = [taps_v_ref[k : k + 1, :] for k in range(KERNEL)]
    skip = taps_v_ref[KERNEL + 1 : KERNEL + 2, :]
    x = v_ref[...]
    total = conv_forward(x, masks, taps, taps_v_ref[KERNEL : KERNEL + 1, :])
    values, dvalues = silu_parts(total)
    decays, stepx, steps, low, lane = pair_decays(pair, run_ref, runt_ref, step_ref)
    affinity = affinity_ref[...]
    ds = ds_ref[...]
    dsb = ds.astype(BF)
    fed = (stepx * values).astype(BF)
    daff = daff_ref[...]
    backs = []
    for e in range(2):
        backs.append(mm((decays[e] * affinity).astype(BF), dsb, TN))
        chosen = jnp.where(low if e == 0 else ~low, ds, 0.0).astype(BF)
        daff = daff + mm(chosen, fed, NT) * decays[e]
    daff_ref[...] = daff
    back = jnp.where(low, backs[0], backs[1])
    inner = scanned_ref[...] - skip * values
    direct = back * values
    moved = dsb.astype(F32) * inner - fed.astype(F32) * back
    dstep, drun = dstep_ref[...], drun_ref[...]
    for e in range(2):
        half = low if e == 0 else ~low
        spot = lane == 2 * pair + e
        dstep = dstep + jnp.where(spot, jnp.sum(jnp.where(half, direct, 0.0), axis=1, keepdims=True), 0.0)
        drun = drun + jnp.where(spot, jnp.sum(jnp.where(half, moved, 0.0), axis=1, keepdims=True), 0.0)
    dstep_ref[...] = dstep
    drun_ref[...] = drun
    dact = stepx * back + skip * ds
    dtotal = dact * dvalues
    dx, tap_grads = conv_backward(dtotal, x, masks, taps)
    gv_ref[...] = dx.astype(BF)
    rows = tap_grads + [
        jnp.sum(dtotal, axis=0, keepdims=True),
        jnp.sum(ds * values, axis=0, keepdims=True),
        jnp.zeros((2, LANES), F32),
    ]
    at = pl.ds(pl.multiple_of(pair * LANES, LANES), LANES)
    vsum_ref[:, at] = vsum_ref[:, at] + jnp.concatenate(rows, axis=0)

    @pl.when(pair == pl.num_programs(1) - 1)
    def _():
        full = daff_ref[...] * allowed_ref[...]
        keys, queries = keys_ref[...], queries_ref[...]
        dqueries = mm_full(full, keys, NN)
        dkeys = mm_full(full, queries, TN)
        for c, dside in enumerate((dkeys, dqueries)):
            lanes = slice(c * LANES, (c + 1) * LANES)
            taps_c = [taps_s_ref[k : k + 1, lanes] for k in range(KERNEL)]
            dsum = dside * silu_parts(sum_ref[:, lanes])[1]
            dside_x, taps_g = conv_backward(dsum, shared_ref[:, lanes], masks, taps_c)
            gs_ref[:, lanes] = dside_x.astype(BF)
            more = taps_g + [jnp.sum(dsum, axis=0, keepdims=True), jnp.zeros((3, LANES), F32)]
            ssum_ref[:, lanes] = ssum_ref[:, lanes] + jnp.concatenate(more, axis=0)
        ddecay = mm_full(lower_ref[...], drun_ref[...], TN)
        rate = -head_ref[1:2, :]
        step = step_ref[...]
        draw = (dstep_ref[...] + ddecay * rate) * jax.nn.sigmoid(raw_ref[...])
        draw = draw * head_ref[2:3, :]
        span = draw.shape[0]
        gs_ref[:, 2 * LANES :] = pltpu.roll(draw, place_ref[0] * per, 1).astype(BF)
        heads = [
            jnp.sum(draw, axis=0, keepdims=True),
            jnp.sum(ddecay * (rate * step), axis=0, keepdims=True) * head_ref[2:3, :],
            jnp.zeros((6, LANES), F32),
        ]
        ssum_ref[:, 2 * LANES :] = ssum_ref[:, 2 * LANES :] + jnp.concatenate(heads, axis=0)


def normgrad_kernel(groups, gz_ref, gv_ref, gs_ref, weight_ref, *outs):
    span = outs[0].shape[0]
    inner = gz_ref.shape[1]
    wz = weight_ref[:, :inner]
    wv = weight_ref[:, inner : 2 * inner]
    ws = weight_ref[:, 2 * inner :]
    for r in range(groups):
        at = slice(r * span, (r + 1) * span)
        total = mm(gz_ref[at, :], wz, NT) + mm(gv_ref[at, :], wv, NT) + mm(gs_ref[at, :], ws, NT)
        outs[r][...] = total.astype(outs[r].dtype)


def final_kernel(groups, width, *refs):
    outs = refs[:groups]
    grads = refs[groups : 2 * groups]
    sums = refs[2 * groups : 3 * groups]
    tokens_ref, cot_ref, gain_ref, output_ref, tgrad_ref, gnorm_ref = refs[3 * groups :]
    factor = gate_scales([s[...] for s in sums], width)[0]
    x = tokens_ref[...].astype(F32)
    total = outs[0][...].astype(F32)
    for part in outs[1:]:
        total = total + part[...].astype(F32)
    output_ref[...] = (x + total * factor[:, 0:1]).astype(BF)
    grad = grads[0][...].astype(F32)
    for part in grads[1:]:
        grad = grad + part[...].astype(F32)
    scale = lax.rsqrt(jnp.mean(x * x, axis=-1, keepdims=True) + EPSILON)
    gained = grad * gain_ref[...]
    bend = scale * scale * scale * jnp.mean(gained * x, axis=-1, keepdims=True)
    tgrad_ref[...] = (cot_ref[...].astype(F32) + (gained * scale - x * bend)).astype(BF)
    gnorm_ref[...] = jnp.broadcast_to(jnp.sum(grad * (x * scale), axis=0, keepdims=True), gnorm_ref.shape)


def place_kernel(groups, place_ref, zk, zs, vk, vs, sk, ss, ok, os, gin_ref, gout_ref):
    member, core = place_ref[0], place_ref[1]
    half = zk.shape[1]
    wide_ = zk.shape[2]
    edge = 2 * groups * wide_
    tail = gin_ref.shape[1] - edge
    for which, (z, v, s, o) in enumerate(((zk, vk, sk, ok), (zs, vs, ss, os))):
        part = core if which == 0 else 1 - core
        rows = pl.ds(pl.multiple_of(part * half, 16), half)
        for k in range(groups):
            col = jnp.bitwise_xor(member, k) * wide_
            gin_ref[rows, pl.ds(pl.multiple_of(col, LANES), wide_)] = z[k].astype(F32)
            gin_ref[rows, pl.ds(pl.multiple_of(groups * wide_ + col, LANES), wide_)] = v[k].astype(F32)
        gin_ref[rows, edge:] = s[:, :tail].astype(F32)
        deep = o.shape[0]
        gout_ref[pl.ds(pl.multiple_of(part * deep, 16), deep), :] = o[...].astype(F32)


def swap(value, axis, step):
    size = lax.axis_size(axis)
    return lax.ppermute(value, axis, [(i, i ^ step) for i in range(size)])


def rounded_sum(a, b):
    return (a.astype(F32) + b.astype(F32)).astype(BF)


def line_sum(value):
    size = lax.axis_size("rep")
    bits = size.bit_length() - 1
    last = bits - 2 if bits >= 3 else bits
    for b in range(1, last):
        value = rounded_sum(value, swap(value, "rep", 1 << b))
    if bits < 3:
        return value
    low = size // 4
    where = lax.axis_index("rep") // low
    inward = [(low * a + i, low * b + i) for a, b in ((0, 1), (3, 2)) for i in range(low)]
    middle = [(low * a + i, low * b + i) for a, b in ((1, 2), (2, 1)) for i in range(low)]
    outward = [(low * a + i, low * b + i) for a, b in ((1, 0), (2, 3)) for i in range(low)]
    value = rounded_sum(value, lax.ppermute(value, "rep", inward))
    value = rounded_sum(value, lax.ppermute(value, "rep", middle))
    back = lax.ppermute(value, "rep", outward)
    return jnp.where((where == 0) | (where == 3), back, value)


def all_sum(value):
    for axis in ("rep", "fsdp"):
        step = 1
        while step < lax.axis_size(axis):
            value = value + swap(value, axis, step)
            step *= 2
    return value


def pick(value, index):
    return lax.dynamic_index_in_dim(value, index, 0, keepdims=False)


def owner_terms(term, groups, member, core, after=None):
    rows = term.shape[0] // (2 * groups)
    cut = term.astype(BF).reshape(groups, 2, rows, term.shape[1])
    kept = lax.dynamic_index_in_dim(cut, core, 1, keepdims=False)
    given = lax.dynamic_index_in_dim(cut, 1 - core, 1, keepdims=False)
    total = rounded_sum(kept, swap(given, "rep", 1))
    return [pick(total, member)] + [
        swap(pick(total, member ^ k), "fsdp", k) for k in range(1, groups)
    ]


def body(
    tokens,
    segment_ids,
    cotangent,
    norm_gain,
    in_weight,
    conv_weight,
    conv_bias,
    step_bias,
    rate_log,
    skip_gain,
    gate_gain,
    out_weight,
):
    groups = lax.axis_size("fsdp")
    member = lax.axis_index("fsdp")
    core = lax.axis_index("rep") % 2
    span, model = tokens.shape
    per = HEADS // groups
    inner = per * HEADDIM
    full = inner * groups
    conv = conv_bias.shape[0] * groups
    tail = in_weight.shape[1] - 2 * full
    padded = -(-tail // 384) * 384
    width = 2 * inner + padded
    pairs = per // 2
    whole = groups * span
    place = jnp.stack([member, core]).astype(jnp.int32)

    pieces = [norm_gain, conv_weight.reshape(-1), conv_bias, segment_ids[0].astype(BF)]
    packed = jnp.concatenate(pieces).reshape(1, -1)
    small = [packed] + [swap(packed, "fsdp", k) for k in range(1, groups)]
    xs = [tokens] + [swap(tokens, "fsdp", k) for k in range(1, groups)]
    rows = in_weight.shape[0]
    shared_w = jnp.pad(in_weight[:, 2 * full :], ((0, 0), (0, padded - tail)))

    def columns_for(peer, source, shared):
        return jnp.concatenate(
            [
                lax.dynamic_slice_in_dim(source, peer * inner, inner, 1),
                lax.dynamic_slice_in_dim(source, full + peer * inner, inner, 1),
                shared,
            ],
            axis=1,
        )

    mine = columns_for(member, in_weight, shared_w)
    half_w = lax.dynamic_slice_in_dim(in_weight, core * (rows // 2), rows // 2, 0)
    half_s = lax.dynamic_slice_in_dim(shared_w, core * (rows // 2), rows // 2, 0)
    near = [swap(columns_for(member ^ k, half_w, half_s), "fsdp", k) for k in range(1, groups)]
    far = [swap(n, "rep", 1) for n in near]
    late, _ = lax.optimization_barrier((cotangent, (near[-1], xs[-1])))
    cots = [cotangent] + [swap(late, "fsdp", k) for k in range(1, groups)]

    table = jnp.concatenate(small, axis=0)
    order = jnp.arange(groups) ^ member
    table = jnp.take(table, order, axis=0).astype(F32)
    taken = rows
    gain_full = table[:, :rows].reshape(1, model)
    cols = conv // groups
    taps_full = jnp.concatenate(
        [
            jnp.swapaxes(table[:, rows : rows + KERNEL * cols].reshape(groups, KERNEL, cols), 0, 1).reshape(
                KERNEL, conv
            ),
            table[:, rows + KERNEL * cols : rows + (KERNEL + 1) * cols].reshape(1, conv),
        ],
        axis=0,
    )
    own_heads = lambda v: lax.dynamic_slice_in_dim(v.astype(F32), member * per, per, 0)
    taps_v = jnp.concatenate(
        [
            lax.dynamic_slice_in_dim(taps_full, member * inner, inner, 1),
            jnp.repeat(own_heads(skip_gain), HEADDIM).reshape(1, inner),
            gate_gain.astype(F32).reshape(1, inner),
            jnp.zeros((1, inner), F32),
        ],
        axis=0,
    )
    taps_s = jnp.concatenate([taps_full[:, full:], jnp.zeros((3, conv - full), F32)], axis=0)
    spread = lambda v: jnp.pad(v, (0, LANES - per)).reshape(1, LANES)
    heads = jnp.concatenate(
        [
            spread(own_heads(step_bias)),
            spread(jnp.exp(own_heads(rate_log))),
            spread(jnp.ones((per,), F32)),
            jnp.zeros((5, LANES), F32),
        ],
        axis=0,
    )
    segs = jnp.concatenate([jnp.broadcast_to(s[:, -span:], (8, span)) for s in small], axis=0).astype(F32)

    sems = pltpu.SemaphoreType.DMA((2 * groups,))
    smem = pl.BlockSpec(memory_space=pltpu.SMEM)
    normed, projected, weight = call(
        partial(inproj_kernel, groups),
        (
            jax.ShapeDtypeStruct((whole, model), BF),
            jax.ShapeDtypeStruct((whole, width), F32),
            jax.ShapeDtypeStruct((model, width), BF),
        ),
        2 * whole * model * width,
        4 * whole * width + 4 * model * width + 4 * whole * model,
        in_specs=[VM] * groups + [VM, smem] + [HBM] * (2 * groups - 1),
        out_specs=(VM, VM, VM),
        scratch_shapes=[sems],
    )(*xs, gain_full, place, mine, *near, *far)

    tile = lambda col: pl.BlockSpec((span, LANES), lambda r, p: (r, col + p))
    per_row = lambda cols_, col: pl.BlockSpec((span, cols_), lambda r, p: (r, col))
    fixed = lambda shape: pl.BlockSpec(shape, lambda r, p: (0, 0))
    pair_cols = pl.BlockSpec((8, LANES), lambda r, p: (0, p))
    seg_spec = pl.BlockSpec((8, span), lambda r, p: (r, 0))
    shared_spec = per_row(padded, 2 * inner // padded)
    state = [
        pltpu.VMEM((KERNEL - 1, span, LANES), F32),
        pltpu.VMEM((span, span), F32),
        pltpu.VMEM((span, LANES), F32),
        pltpu.VMEM((span, LANES), F32),
        pltpu.VMEM((LANES, span), F32),
    ]
    scan_flops = 4 * whole * span * inner
    scanned, gated, squares = call(
        partial(forward_kernel, per),
        (
            jax.ShapeDtypeStruct((whole, inner), F32),
            jax.ShapeDtypeStruct((whole, inner), BF),
            jax.ShapeDtypeStruct((8 * groups, span), F32),
        ),
        8 * scan_flops,
        16 * whole * inner,
        grid=(groups, pairs),
        in_specs=[
            smem,
            tile(0),
            tile(pairs),
            shared_spec,
            seg_spec,
            fixed((8, conv - full)),
            pair_cols,
            fixed((8, LANES)),
        ],
        out_specs=(tile(0), tile(0), seg_spec),
        scratch_shapes=state + [pltpu.VMEM((span, LANES), F32)],
    )(place, projected, projected, projected, segs, taps_s, taps_v, heads)

    proj_flops = 2 * whole * inner * model
    dm, sums = call(
        partial(mixgrad_kernel, groups),
        (jax.ShapeDtypeStruct((whole, inner), F32), jax.ShapeDtypeStruct((8 * groups, span), F32)),
        proj_flops,
        2 * whole * model + 6 * whole * inner + 2 * inner * model,
        in_specs=[VM] * (groups + 3),
        out_specs=(VM, VM),
    )(*cots, out_weight, gated, squares)
    sums_all = [sums] + [swap(sums, "fsdp", k) for k in range(1, groups)]

    outs = call(
        partial(outproj_kernel, groups),
        tuple(jax.ShapeDtypeStruct((span, model), BF if k else F32) for k in range(groups)),
        proj_flops,
        2 * whole * model + 2 * whole * inner + 2 * inner * model,
        in_specs=[VM, VM],
        out_specs=(VM,) * groups,
    )(gated, out_weight)
    outs = [outs[0]] + [swap(outs[k], "fsdp", k) for k in range(1, groups)]

    row_spec = lambda cols_, col=0: pl.BlockSpec((span, cols_), lambda r: (r, col))
    gz, ds, mixed, gate_sum = call(
        partial(gatebwd_kernel, groups, float(full)),
        (
            jax.ShapeDtypeStruct((whole, inner), BF),
            jax.ShapeDtypeStruct((whole, inner), F32),
            jax.ShapeDtypeStruct((whole, inner), BF),
            jax.ShapeDtypeStruct((8, inner), F32),
        ),
        20 * whole * inner,
        20 * whole * inner,
        grid=(groups,),
        in_specs=[
            pl.BlockSpec((8, span), (lambda k: lambda r: (jnp.bitwise_xor(r, k), 0))(k)) for k in range(groups)
        ]
        + [row_spec(inner), row_spec(inner), row_spec(inner), pl.BlockSpec((8, inner), lambda r: (0, 0))],
        out_specs=(
            row_spec(inner),
            row_spec(inner),
            row_spec(inner),
            pl.BlockSpec((8, inner), lambda r: (0, 0)),
        ),
    )(*sums_all, projected, scanned, dm, jnp.broadcast_to(gate_gain.astype(F32).reshape(1, inner), (8, inner)))

    cot_all = jnp.concatenate(cots, axis=0)
    grad_out = lax.dot_general(mixed, cot_all, TN, preferred_element_type=F32).astype(BF)
    grad_z = lax.dot_general(normed, gz, TN, preferred_element_type=F32)
    cut = grad_out.reshape(2, inner // 2, model)
    out_part = rounded_sum(pick(cut, core), swap(pick(cut, 1 - core), "rep", 1))
    out_part = line_sum(out_part)
    out_other = swap(out_part, "rep", 1)
    z_part = line_sum(jnp.stack(owner_terms(grad_z, groups, member, core)))
    z_other = swap(z_part, "rep", 1)

    gv, gs, vsum, ssum = call(
        partial(backward_kernel, per),
        (
            jax.ShapeDtypeStruct((whole, inner), BF),
            jax.ShapeDtypeStruct((whole, padded), BF),
            jax.ShapeDtypeStruct((8, inner), F32),
            jax.ShapeDtypeStruct((8, padded), F32),
        ),
        16 * scan_flops,
        16 * whole * inner,
        grid=(groups, pairs),
        in_specs=[
            smem,
            tile(0),
            tile(pairs),
            tile(0),
            shared_spec,
            seg_spec,
            fixed((8, conv - full)),
            pair_cols,
            fixed((8, LANES)),
        ],
        out_specs=(tile(0), per_row(padded, 0), fixed((8, inner)), fixed((8, padded))),
        scratch_shapes=state
        + [
            pltpu.VMEM((span, span), F32),
            pltpu.VMEM((span, span), F32),
            pltpu.VMEM((span, LANES), F32),
            pltpu.VMEM((span, 2 * LANES), F32),
            pltpu.VMEM((span, LANES), F32),
            pltpu.VMEM((span, LANES), F32),
            pltpu.VMEM((span, span), F32),
            pltpu.VMEM((span, LANES), F32),
            pltpu.VMEM((span, LANES), F32),
        ],
    )(place, ds, projected, scanned, projected, segs, taps_s, taps_v, heads)

    backs = call(
        partial(normgrad_kernel, groups),
        tuple(jax.ShapeDtypeStruct((span, model), BF if k else F32) for k in range(groups)),
        2 * whole * width * model,
        2 * whole * model + 2 * whole * width + 2 * width * model,
        in_specs=[VM] * 4,
        out_specs=(VM,) * groups,
    )(gz, gv, gs, weight)
    backs = [backs[0]] + [swap(backs[k], "fsdp", k) for k in range(1, groups)]

    grad_v = lax.dot_general(normed, gv, TN, preferred_element_type=F32)
    v_part = line_sum(jnp.stack(owner_terms(grad_v, groups, member, core)))
    v_other = swap(v_part, "rep", 1)
    grad_s = lax.dot_general(normed, gs, TN, preferred_element_type=F32)
    s_terms = owner_terms(grad_s, groups, member, core)
    s_part = s_terms[0].astype(F32)
    for term in s_terms[1:]:
        s_part = s_part + term.astype(F32)
    s_part = line_sum(s_part.astype(BF))
    s_other = swap(s_part, "rep", 1)

    whole_spec = lambda shape: pl.BlockSpec(shape, lambda i: (0,) * len(shape))
    output, tokens_grad, norm_sum = call(
        partial(final_kernel, groups, float(full)),
        (
            jax.ShapeDtypeStruct((span, model), BF),
            jax.ShapeDtypeStruct((span, model), BF),
            jax.ShapeDtypeStruct((8, model), F32),
        ),
        30 * span * model,
        24 * span * model,
        grid=(1,),
        in_specs=[whole_spec((span, model))] * (2 * groups)
        + [pl.BlockSpec((8, span), (lambda k: lambda i: (k, 0))(k)) for k in range(groups)]
        + [whole_spec((span, model))] * 2
        + [whole_spec((1, model))],
        out_specs=(whole_spec((span, model)), whole_spec((span, model)), whole_spec((8, model))),
    )(*outs, *backs, *sums_all, tokens, cotangent, gain_full)

    grad_inproj, grad_outproj = call(
        partial(place_kernel, groups),
        (
            jax.ShapeDtypeStruct(in_weight.shape, F32),
            jax.ShapeDtypeStruct(out_weight.shape, F32),
        ),
        in_weight.size,
        6 * (in_weight.size + out_weight.size),
        in_specs=[smem] + [VM] * 8,
        out_specs=(VM, VM),
    )(place, z_part, z_other, v_part, v_other, s_part, s_other, out_part, out_other)

    own_cols = lambda v: lax.dynamic_update_slice_in_dim(
        jnp.zeros((v.shape[0], full), F32), v, member * inner, 1
    )
    own_spot = lambda v: lax.dynamic_update_slice_in_dim(jnp.zeros((HEADS,), F32), v, member * per, 0)
    taps_grad = jnp.concatenate([own_cols(vsum[: KERNEL + 1]), ssum[: KERNEL + 1, : conv - full]], axis=1)
    head_grads = [
        own_spot(ssum[0, 2 * LANES : 2 * LANES + per]),
        own_spot(ssum[1, 2 * LANES : 2 * LANES + per]),
        own_spot(vsum[KERNEL + 1].reshape(per, HEADDIM).sum(axis=1)),
    ]
    flat = jnp.concatenate(
        [norm_sum[0], taps_grad.reshape(-1), own_cols(gate_sum[:1]).reshape(-1)] + head_grads
    )
    length = flat.shape[0]
    flat = jnp.pad(flat, (0, -length % 1024)).reshape(-1, LANES)
    flat = all_sum(flat).reshape(-1)
    at = 0
    grad_norm = lax.dynamic_slice_in_dim(flat, member * rows, rows, 0)
    at += model
    taps_all = flat[at : at + (KERNEL + 1) * conv].reshape(KERNEL + 1, conv)
    taps_own = lax.dynamic_slice_in_dim(taps_all, member * cols, cols, 1)
    at += (KERNEL + 1) * conv
    grad_gate = lax.dynamic_slice_in_dim(flat, at + member * inner, inner, 0)
    at += full
    return (
        output,
        tokens_grad,
        grad_norm,
        grad_inproj,
        taps_own[:KERNEL],
        taps_own[KERNEL],
        flat[at : at + HEADS],
        flat[at + HEADS : at + 2 * HEADS],
        flat[at + 2 * HEADS : at + 3 * HEADS],
        grad_gate,
        grad_outproj,
    )


def solution(mesh):
    rows = P(("rep", "fsdp"), None)
    in_specs = (
        rows,
        rows,
        rows,
        P("fsdp"),
        P("fsdp", None),
        P(None, "fsdp"),
        P("fsdp"),
        P(),
        P(),
        P(),
        P("fsdp"),
        P("fsdp", None),
    )
    out_specs = (
        rows,
        rows,
        P("fsdp"),
        P("fsdp", None),
        P(None, "fsdp"),
        P("fsdp"),
        P(),
        P(),
        P(),
        P("fsdp"),
        P("fsdp", None),
    )
    return jax.shard_map(body, mesh=mesh, in_specs=in_specs, out_specs=out_specs, check_vma=False)
```

time: 1210 us -> 527 us (0.44)
  waiting for transfers between devices: 871 us -> 203 us
  Pallas kernels: 0 us -> 141 us
  matrix products: 131 us -> 14.7 us
  blocking collectives: 79.1 us -> 0 us
  starting transfers between devices: 0.28 us -> 67.4 us
  other arithmetic: 59.4 us -> 35 us
  local copies, waits for them, and re-layouts: 43.5 us -> 62.6 us
  between operations: 18.3 us -> 1.93 us
    reduce_scatter x2 -> x0, waiting for transfers between devices: 458 us -> none  [the longest x1 369 us: body(): lax.psum_scatter(pieces[1], ('rep', 'fsdp'), scatter_dimension=0, tiled=T...]
    all_gather x4 -> x0, waiting for transfers between devices: 293 us -> none  [the longest x1 147 us: body(): lax.all_gather(in_weight, 'fsdp', axis=0, tiled=True)]
    ppermute x0 -> x58, waiting for transfers between devices: none -> 203 us  [the longest x46 140 us: swap(): return lax.ppermute(value, axis, [(i, i ^ step) for i in range(size)])]
    pallas_call x0 -> x9, Pallas kernels: none -> 141 us  [the longest x1 48.2 us: body(): call(partial(backward_kernel, per), (jax.ShapeDtypeStruct((whole, inner),...]
    unnamed x8 -> x0, waiting for transfers between devices: 120 us -> none
    dot_general x16 -> x4, matrix products: 131 us -> 14.7 us  [the longest x1 4.74 us: body(): grad_z = lax.dot_general(normed, gz, TN, preferred_element_type=F32)]
    ppermute x0 -> x58, starting transfers between devices: none -> 67.4 us  [the longest x46 43.5 us: swap(): return lax.ppermute(value, axis, [(i, i ^ step) for i in range(size)])]
    unnamed x2 -> x0, blocking collectives: 40 us -> none
  transfers between devices with their start and end apart: 7 -> 58, of which waited for: 7 -> 17; matrix products, arithmetic and copies ran while one was open for 16% -> 16% of each run, Pallas kernels for 0% -> 13%
where the time goes in v1:
time: 527 us; the launch traced here: 525 us
  waiting for transfers between devices  203 us (39%)
  Pallas kernels  141 us (27%)
  starting transfers between devices  67.4 us (13%)
  local copies, waits for them, and re-layouts  62.6 us (12%)
  other arithmetic  35 us (7%)
  matrix products  14.7 us (3%)
    ppermute x46, waiting for transfers between devices, swap(): return lax.ppermute(value, axis, [(i, i ^ step) for i in range(size)])  140 us
    ppermute x4, waiting for transfers between devices, line_sum(): back = lax.ppermute(value, 'rep', outward)  62.5 us
    pallas_call x1, Pallas kernels, body(): call(partial(backward_kernel, per), (jax.ShapeDtypeStruct((whole, inner),...  48.2 us
    ppermute x46, starting transfers between devices, swap(): return lax.ppermute(value, axis, [(i, i ^ step) for i in range(size)])  43.5 us
    unnamed x130, local copies, waits for them, and re-layouts  26.3 us
    pallas_call x1, Pallas kernels, body(): call(partial(forward_kernel, per), (jax.ShapeDtypeStruct((whole, inner),...  25.5 us
    pallas_call x1, Pallas kernels, body(): call(partial(inproj_kernel, groups), (jax.ShapeDtypeStruct((whole, model)...  19.1 us
    convert_element_type x12, other arithmetic, rounded_sum(): return (a.astype(F32) + b.astype(F32)).astype(BF)  17.2 us
  transfers between devices with their start and end apart: 58, of which 17 were waited for; matrix products, arithmetic and copies ran while one was open for 16% of the time, Pallas kernels for 13%

profile of v1, /device:TPU:0, one launch (start us, length us, event | category | flops | bytes accessed | tf_op | source)
XLA Modules:
  0.0 524.9 jit_solution(2276692195564744617)
XLA Ops:
  0.6 3.0 collective-permute-start
  3.7 1.5 collective-permute-start.2
  10.1 1.5 collective-permute-start.4
  17.6 3.8 fusion.19
  29.2 11.0 %collective-permute-done.5 = bf16[1,4800]{1,0:T(2,128)(2,1)} collective-permute-done((bf16[1,4800]{1,0:T(2,128)(2,1)}, bf16[1,4800]{1,0:T(2,128)(2,1)}, u32[]{:S(2)}, u32[]{:S(2)}) %collective-permute-start.5) | collective-permute-done | bytes 9632 | tf_op jit(solution)/shard_map/ppermute | solution.py:472
  40.2 1.5 collective-permute-start.6
  42.2 1.5 collective-permute-start.8
  46.9 13.0 %collective-permute-done.6.refs_7_ = bf16[192,1920]{1,0:T(8,128)(2,1)} collective-permute-done((bf16[192,1920]{1,0:T(8,128)(2,1)}, bf16[192,1920]{1,0:T(8,128)(2,1)}, u32[]{:S(2)}, u32[]{:S(2)}) %collective-permute-start.6) | collective-permute-done | bytes 737312 | tf_op jit(solution)/shard_map/ppermute | solution.py:472
  60.2 16.4 %collective-permute-done.7.refs_8_ = bf16[192,1920]{1,0:T(8,128)(2,1)} collective-permute-done((bf16[192,1920]{1,0:T(8,128)(2,1)}, bf16[192,1920]{1,0:T(8,128)(2,1)}, u32[]{:S(2)}, u32[]{:S(2)}) %collective-permute-start.7) | collective-permute-done | bytes 737312 | tf_op jit(solution)/shard_map/ppermute | solution.py:472
  80.8 10.6 %collective-permute-done.1.refs_2_ = bf16[256,1536]{1,0:T(8,128)(2,1)S(1)} collective-permute-done((bf16[256,1536]{1,0:T(8,128)(2,1)S(1)}, bf16[256,1536]{1,0:T(8,128)(2,1)S(1)}, u32[]{:S(2)}, u32[]{:S(2)}) %collective-permute-start.1) | collective-permute-done | bytes 786464 | tf_op jit(solution)/shard_map/ppermute | solution.py:472
  95.4 19.1 %shard_map.203 = (bf16[1024,1536]{1,0:T(8,128)(2,1)}, f32[1024,1920]{1,0:T(8,128)}, bf16[1536,1920]{1,0:T(8,128)(2,1)}) custom-call(bf16[256,1536]{1,0:T(8,128)(2,1)} %refs_12_.1, bf16[256,1536]{1,0:T(8,128)(2,1)} %collective-permute-done.refs_1_, bf16[256,1536]{1,0:T(8,128)(2,1)} %copy-done.50, bf16[256,1536]{1,0:T(8,128)(2,1)} %collective-permute-done.2.refs_3_, ...), custom_call_target="tpu_custom_call" | custom-call | flops 6039797760 | bytes 25952256 | tf_op jit(solution)/shard_map/pallas_call | solution.py:616
  114.5 25.5 %shard_map.204 = (f32[1024,768]{1,0:T(8,128)}, bf16[1024,768]{1,0:T(8,128)(2,1)}, f32[32,256]{1,0:T(8,128)}) custom-call(s32[2]{0:T(128)} %pad_add_fusion.refs_5_.place_ref, f32[1024,1920]{1,0:T(8,128)} %get-tuple-element.41.z_ref.v_ref.shared_ref.refs_4_, f32[1024,1920]{1,0:T(8,128)} %get-tuple-element.41.z_ref.v_ref.shared_ref.refs_4_, ...), custom_call_target="tpu_custom_call" | custom-call | flops 6442450944 | bytes 12582912 | tf_op jit(solution)/shard_map/pallas_call | solution.py:644
  141.4 7.5 %shard_map.206 = (f32[1024,768]{1,0:T(8,128)}, f32[32,256]{1,0:T(8,128)}) custom-call(bf16[256,1536]{1,0:T(8,128)(2,1)} %refs_13_.1, bf16[256,1536]{1,0:T(8,128)(2,1)} %copy-done.44, bf16[256,1536]{1,0:T(8,128)(2,1)} %copy-done.46, bf16[256,1536]{1,0:T(8,128)(2,1)} %copy-done.48, bf16[768,1536]{1,0:T(8,128)(2,1)} %refs_4_.1, ...), custom_call_target="tpu_custom_call" | custom-call | flops 2415919104 | bytes 10223616 | tf_op jit(solution)/shard_map/pallas_call | solution.py:669
  149.0 1.5 collective-permute-start.18
  152.5 5.7 %shard_map.205 = (f32[256,1536]{1,0:T(8,128)}, bf16[256,1536]{1,0:T(8,128)(2,1)}, bf16[256,1536]{1,0:T(8,128)(2,1)}, bf16[256,1536]{1,0:T(8,128)(2,1)}) custom-call(bf16[1024,768]{1,0:T(8,128)(2,1)} %get-tuple-element.42.gated_ref.refs_5_, bf16[768,1536]{1,0:T(8,128)(2,1)} %refs_4_.1), custom_call_target="tpu_custom_call" | custom-call | flops 2415919104 | bytes 7077888 | tf_op jit(solution)/shard_map/pallas_call | solution.py:679
  158.8 7.6 %shard_map.207 = (bf16[1024,768]{1,0:T(8,128)(2,1)}, f32[1024,768]{1,0:T(8,128)}, bf16[1024,768]{1,0:T(8,128)(2,1)}, f32[8,768]{1,0:T(8,128)}) custom-call(f32[32,256]{1,0:T(8,128)} %get-tuple-element.49.refs_0_.refs_8_, f32[32,256]{1,0:T(8,128)} %copy-done.32, f32[32,256]{1,0:T(8,128)} %copy-done.33, f32[32,256]{1,0:T(8,128)} %copy-done.34, ...), custom_call_target="tpu_custom_call" | custom-call | flops 15728640 | bytes 15728640 | tf_op jit(solution)/shard_map/pallas_call | solution.py:690
  166.4 48.2 %shard_map.208 = (bf16[1024,768]{1,0:T(8,128)(2,1)}, bf16[1024,384]{1,0:T(8,128)(2,1)}, f32[8,768]{1,0:T(8,128)}, f32[8,384]{1,0:T(8,128)}) custom-call(s32[2]{0:T(128)} %pad_add_fusion.refs_5_.place_ref, f32[1024,768]{1,0:T(8,128)} %get-tuple-element.53.ds_ref, f32[1024,1920]{1,0:T(8,128)} %get-tuple-element.41.z_ref.v_ref.shared_ref.refs_4_, ...), custom_call_target="tpu_custom_call" | custom-call | flops 12884901888 | bytes 12582912 | tf_op jit(solution)/shard_map/pallas_call | solution.py:723
  215.3 4.7 convolution_convert_fusion.2
  220.3 2.1 copy-done.58
  222.3 2.9 convolution_convert_fusion.1
  227.4 2.9 convolution_convert_fusion
  232.9 11.5 %shard_map.209 = (f32[256,1536]{1,0:T(8,128)}, bf16[256,1536]{1,0:T(8,128)(2,1)}, bf16[256,1536]{1,0:T(8,128)(2,1)}, bf16[256,1536]{1,0:T(8,128)(2,1)}) custom-call(bf16[1024,768]{1,0:T(8,128)(2,1)} %get-tuple-element.52.gz_ref, bf16[1024,768]{1,0:T(8,128)(2,1)} %get-tuple-element.54.gv_ref, bf16[1024,384]{1,0:T(8,128)(2,1)} %get-tuple-element.55.gs_ref, ...), custom_call_target="tpu_custom_call" | custom-call | flops 6039797760 | bytes 12976128 | tf_op jit(solution)/shard_map/pallas_call | solution.py:760
  244.4 4.1 convolution_convert_fusion.3
  249.8 1.6 fusion.9
  251.5 1.8 collective-permute-start.32
  255.1 1.6 fusion.7
  256.6 3.6 collective-permute-start.54
  260.2 1.6 fusion.8
  262.9 1.5 collective-permute-start.12
  265.2 2.6 collective-permute-done.31
  267.8 1.7 collective-permute-start.40
  271.6 19.5 %collective-permute-done.40 = bf16[192,768]{1,0:T(8,128)(2,1)S(1)} collective-permute-done((bf16[192,768]{1,0:T(8,128)(2,1)S(1)}, bf16[192,768]{1,0:T(8,128)(2,1)S(1)}, u32[]{:S(2)}, u32[]{:S(2)}) %collective-permute-start.40) | collective-permute-done | bytes 294944 | tf_op jit(solution)/shard_map/ppermute | solution.py:472
  291.0 1.5 collective-permute-start.38
  293.7 3.5 collective-permute-done.39
  297.2 3.5 collective-permute-start.33
  301.0 1.8 collective-permute-start.14
  306.9 2.5 collective-permute-start.41
  309.7 12.8 %collective-permute-done.14.refs_3_ = bf16[256,1536]{1,0:T(8,128)(2,1)S(1)} collective-permute-done((bf16[256,1536]{1,0:T(8,128)(2,1)S(1)}, bf16[256,1536]{1,0:T(8,128)(2,1)S(1)}, u32[]{:S(2)}, u32[]{:S(2)}) %collective-permute-start.14) | collective-permute-done | bytes 786464 | tf_op jit(solution)/shard_map/ppermute | solution.py:472
  323.4 1.7 collective-permute-start.55
  325.9 1.5 reshape.127
  333.3 17.6 %collective-permute-done.46 = bf16[192,384]{1,0:T(8,128)(2,1)S(1)} collective-permute-done((bf16[192,384]{1,0:T(8,128)(2,1)}, bf16[192,384]{1,0:T(8,128)(2,1)S(1)}, u32[]{:S(2)}, u32[]{:S(2)}) %collective-permute-start.46) | collective-permute-done | bytes 147488 | tf_op jit(solution)/shard_map/ppermute | solution.py:472
  352.8 2.2 add_convert_fusion.5
  355.0 1.7 collective-permute-start.34
  356.7 2.6 add_convert_fusion.3
  359.3 1.7 collective-permute-start.42
  361.0 1.8 fusion.13
  362.8 21.5 %collective-permute-done.22.refs_6_ = bf16[256,1536]{1,0:T(8,128)(2,1)} collective-permute-done((bf16[256,1536]{1,0:T(8,128)(2,1)}, bf16[256,1536]{1,0:T(8,128)(2,1)}, u32[]{:S(2)}, u32[]{:S(2)}) %collective-permute-start.22) | collective-permute-done | bytes 786464 | tf_op jit(solution)/shard_map/ppermute | solution.py:472
  384.3 3.4 collective-permute-start.49
  387.7 6.0 %shard_map.210 = (bf16[256,1536]{1,0:T(8,128)(2,1)}, bf16[256,1536]{1,0:T(8,128)(2,1)}, f32[8,1536]{1,0:T(8,128)}) custom-call(f32[256,1536]{1,0:T(8,128)} %get-tuple-element.43.refs_0_, bf16[256,1536]{1,0:T(8,128)(2,1)} %copy-done.27, bf16[256,1536]{1,0:T(8,128)(2,1)} %copy-done.28, bf16[256,1536]{1,0:T(8,128)(2,1)} %copy-done.29, ...), custom_call_target="tpu_custom_call" | custom-call | flops 11796480 | bytes 9437184 | tf_op jit(solution)/shard_map/pallas_call | solution.py:782
  395.1 1.6 concatenate.54
  396.7 1.6 add_convert_fusion
  399.8 1.8 add_convert_fusion.4
  402.9 2.1 add_convert_fusion.2
  406.3 5.9 %collective-permute-start.25 = (f32[168,128]{1,0:T(8,128)S(1)}, f32[168,128]{1,0:T(8,128)S(1)}, u32[]{:S(2)}, u32[]{:S(2)}) collective-permute-start(f32[168,128]{1,0:T(8,128)S(1)} %fusion.18), channel_id=1, source_target_pairs={{0,8},{4,12},{8,0},{12,4},{16,24},{20,28},{24,16},{28,20},{1,9},{5... | collective-permute-start | bytes 258056 | tf_op jit(solution)/shard_map/ppermute | solution.py:472
  414.0 15.1 %collective-permute-done.56 = bf16[384,1536]{1,0:T(8,128)(2,1)S(1)} collective-permute-done((bf16[384,1536]{1,0:T(8,128)(2,1)S(1)}, bf16[384,1536]{1,0:T(8,128)(2,1)S(1)}, u32[]{:S(2)}, u32[]{:S(2)}) %collective-permute-start.56) | collective-permute-done | bytes 1179680 | tf_op jit(solution)/shard_map/ppermute | solution.py:494
  429.3 25.1 %collective-permute-done.35 = bf16[4,192,768]{2,1,0:T(8,128)(2,1)S(1)} collective-permute-done((bf16[4,192,768]{2,1,0:T(8,128)(2,1)S(1)}, bf16[4,192,768]{2,1,0:T(8,128)(2,1)S(1)}, u32[]{:S(2)}, u32[]{:S(2)}) %collective-permute-start.35) | collective-permute-done | bytes 1179680 | tf_op jit(solution)/shard_map/ppermute | solution.py:494
  455.5 22.3 %collective-permute-done.43 = bf16[4,192,768]{2,1,0:T(8,128)(2,1)S(1)} collective-permute-done((bf16[4,192,768]{2,1,0:T(8,128)(2,1)S(1)}, bf16[4,192,768]{2,1,0:T(8,128)(2,1)S(1)}, u32[]{:S(2)}, u32[]{:S(2)}) %collective-permute-start.43) | collective-permute-done | bytes 1179680 | tf_op jit(solution)/shard_map/ppermute | solution.py:494
  480.8 4.1 collective-permute-done.26
  485.8 4.6 collective-permute-done.27
  492.1 1.6 broadcast_select_fusion.3.sk
  493.7 2.2 collective-permute-done.28
  497.8 1.5 reshape.135
  504.6 9.4 %shard_map.211 = (f32[384,6448]{1,0:T(8,128)}, f32[768,1536]{1,0:T(8,128)}) custom-call(s32[2]{0:T(128)} %pad_add_fusion.refs_5_.place_ref, bf16[4,192,768]{2,1,0:T(8,128)(2,1)} %broadcast_select_fusion.2.zk, bf16[4,192,768]{2,1,0:T(8,128)(2,1)} %collective-permute-done.36.zs, bf16[4,192,768]{2,1,0:T(8,128)(2,1)} %copy-done.1, ...), custom_call_target="tpu_custom_call" | custom-call | flops 2476032 | bytes 21934080 | tf_op jit(solution)/shard_map/pallas_call | solution.py:799
  514.0 10.7 %copy.47 = f32[384,6448]{0,1:T(8,128)} copy(f32[384,6448]{1,0:T(8,128)} %get-tuple-element.85) | data formatting | bytes 19808256
  (305 shorter events, 83.4 us)
Async XLA Ops:
  0.6 80.2 %collective-permute-start = (bf16[256,1536]{1,0:T(8,128)(2,1)}, bf16[256,1536]{1,0:T(8,128)(2,1)}, u32[]{:S(2)}, u32[]{:S(2)}) collective-permute-start(bf16[256,1536]{1,0:T(8,128)(2,1)} %refs_12_.1), channel_id=1, source_target_pairs={{0,1},{1,0},{2,3},{3,2},{4,5},{5,4},{6,7},{7,6},{8,9},{9,8},{10,11... | collective-permute-start | bytes 2359304 | tf_op jit(solution)/shard_map/ppermute | solution.py:472
  3.7 73.4 %collective-permute-start.2 = (bf16[256,1536]{1,0:T(8,128)(2,1)}, bf16[256,1536]{1,0:T(8,128)(2,1)}, u32[]{:S(2)}, u32[]{:S(2)}) collective-permute-start(bf16[256,1536]{1,0:T(8,128)(2,1)} %refs_12_.1), channel_id=1, source_target_pairs={{0,3},{1,2},{2,1},{3,0},{4,7},{5,6},{6,5},{7,4},{8,11},{9,10},{10,... | collective-permute-start | bytes 2359304 | tf_op jit(solution)/shard_map/ppermute | solution.py:472
  8.7 31.5 %collective-permute-start.5 = (bf16[1,4800]{1,0:T(2,128)(2,1)}, bf16[1,4800]{1,0:T(2,128)(2,1)}, u32[]{:S(2)}, u32[]{:S(2)}) collective-permute-start(bf16[1,4800]{1,0:T(2,128)(2,1)} %reshape.118), channel_id=1, source_target_pairs={{0,3},{1,2},{2,1},{3,0},{4,7},{5,6},{6,5},{7,4},{8,11},{9,10},{10,... | collective-permute-start | bytes 28808 | tf_op jit(solution)/shard_map/ppermute | solution.py:472
  10.1 31.6 %collective-permute-start.4 = (bf16[1,4800]{1,0:T(2,128)(2,1)}, bf16[1,4800]{1,0:T(2,128)(2,1)}, u32[]{:S(2)}, u32[]{:S(2)}) collective-permute-start(bf16[1,4800]{1,0:T(2,128)(2,1)} %reshape.118), channel_id=1, source_target_pairs={{0,2},{1,3},{2,0},{3,1},{4,6},{5,7},{6,4},{7,5},{8,10},{9,11},{10,... | collective-permute-start | bytes 28808 | tf_op jit(solution)/shard_map/ppermute | solution.py:472
  11.7 30.6 %collective-permute-start.3 = (bf16[1,4800]{1,0:T(2,128)(2,1)}, bf16[1,4800]{1,0:T(2,128)(2,1)}, u32[]{:S(2)}, u32[]{:S(2)}) collective-permute-start(bf16[1,4800]{1,0:T(2,128)(2,1)} %reshape.118), channel_id=1, source_target_pairs={{0,1},{1,0},{2,3},{3,2},{4,5},{5,4},{6,7},{7,6},{8,9},{9,8},{10,11... | collective-permute-start | bytes 28808 | tf_op jit(solution)/shard_map/ppermute | solution.py:472
  26.8 33.1 %copy-start.24 = (bf16[256,1536]{1,0:T(8,128)(2,1)S(1)}, bf16[256,1536]{1,0:T(8,128)(2,1)}, u32[]{:S(2)}) copy-start(bf16[256,1536]{1,0:T(8,128)(2,1)} %refs_12_.1) | copy-start | bytes 2359300
  28.3 52.5 %copy-start.25 = (bf16[256,1536]{1,0:T(8,128)(2,1)S(1)}, bf16[256,1536]{1,0:T(8,128)(2,1)}, u32[]{:S(2)}) copy-start(bf16[256,1536]{1,0:T(8,128)(2,1)} %refs_13_.1) | copy-start | bytes 2359300
  40.2 19.7 %collective-permute-start.6 = (bf16[192,1920]{1,0:T(8,128)(2,1)}, bf16[192,1920]{1,0:T(8,128)(2,1)}, u32[]{:S(2)}, u32[]{:S(2)}) collective-permute-start(bf16[192,1920]{1,0:T(8,128)(2,1)} %get-tuple-element.114), channel_id=1, source_target_pairs={{0,1},{1,0},{2,3},{3,2},{4,5},{5,4},{6,7},{7,6},{8,9},{9,8},{10,11... | collective-permute-start | bytes 2211848 | tf_op jit(solution)/shard_map/ppermute | solution.py:472
  41.7 34.9 %collective-permute-start.7 = (bf16[192,1920]{1,0:T(8,128)(2,1)}, bf16[192,1920]{1,0:T(8,128)(2,1)}, u32[]{:S(2)}, u32[]{:S(2)}) collective-permute-start(bf16[192,1920]{1,0:T(8,128)(2,1)} %get-tuple-element.113), channel_id=1, source_target_pairs={{0,2},{1,3},{2,0},{3,1},{4,6},{5,7},{6,4},{7,5},{8,10},{9,11},{10,... | collective-permute-start | bytes 2211848 | tf_op jit(solution)/shard_map/ppermute | solution.py:472
  42.2 34.4 %collective-permute-start.8 = (bf16[192,1920]{1,0:T(8,128)(2,1)}, bf16[192,1920]{1,0:T(8,128)(2,1)}, u32[]{:S(2)}, u32[]{:S(2)}) collective-permute-start(bf16[192,1920]{1,0:T(8,128)(2,1)} %get-tuple-element.112), channel_id=1, source_target_pairs={{0,3},{1,2},{2,1},{3,0},{4,7},{5,6},{6,5},{7,4},{8,11},{9,10},{10,... | collective-permute-start | bytes 2211848 | tf_op jit(solution)/shard_map/ppermute | solution.py:472
  59.9 31.6 %collective-permute-start.1 = (bf16[256,1536]{1,0:T(8,128)(2,1)S(1)}, bf16[256,1536]{1,0:T(8,128)(2,1)S(1)}, u32[]{:S(2)}, u32[]{:S(2)}) collective-permute-start(bf16[256,1536]{1,0:T(8,128)(2,1)S(1)} %copy-done.24), channel_id=1, source_target_pairs={{0,2},{1,3},{2,0},{3,1},{4,6},{5,7},{6,4},{7,5},{8,10},{9,11},{10,... | collective-permute-start | bytes 2359304 | tf_op jit(solution)/shard_map/ppermute | solution.py:472
  76.6 15.8 %collective-permute-start.9 = (bf16[192,1920]{1,0:T(8,128)(2,1)}, bf16[192,1920]{1,0:T(8,128)(2,1)S(1)}, u32[]{:S(2)}, u32[]{:S(2)}) collective-permute-start(bf16[192,1920]{1,0:T(8,128)(2,1)} %collective-permute-done.6.refs_7_), channel_id=1, source_target_pairs={{0,4},{4,0},{8,12},{12,8},{16,20},{20,16},{24,28},{28,24},{1,5},{5... | collective-permute-start | bytes 2211848 | tf_op jit(solution)/shard_map/ppermute | solution.py:472
  76.6 16.9 %collective-permute-start.10 = (bf16[192,1920]{1,0:T(8,128)(2,1)}, bf16[192,1920]{1,0:T(8,128)(2,1)S(1)}, u32[]{:S(2)}, u32[]{:S(2)}) collective-permute-start(bf16[192,1920]{1,0:T(8,128)(2,1)} %collective-permute-done.7.refs_8_), channel_id=1, source_target_pairs={{0,4},{4,0},{8,12},{12,8},{16,20},{20,16},{24,28},{28,24},{1,5},{5... | collective-permute-start | bytes 2211848 | tf_op jit(solution)/shard_map/ppermute | solution.py:472
  77.1 17.4 %collective-permute-start.11 = (bf16[192,1920]{1,0:T(8,128)(2,1)}, bf16[192,1920]{1,0:T(8,128)(2,1)S(1)}, u32[]{:S(2)}, u32[]{:S(2)}) collective-permute-start(bf16[192,1920]{1,0:T(8,128)(2,1)} %collective-permute-done.8.refs_9_), channel_id=1, source_target_pairs={{0,4},{4,0},{8,12},{12,8},{16,20},{20,16},{24,28},{28,24},{1,5},{5... | collective-permute-start | bytes 2211848 | tf_op jit(solution)/shard_map/ppermute | solution.py:472
  80.8 59.2 %collective-permute-start.15 = (bf16[256,1536]{1,0:T(8,128)(2,1)S(1)}, bf16[256,1536]{1,0:T(8,128)(2,1)S(1)}, u32[]{:S(2)}, u32[]{:S(2)}) collective-permute-start(bf16[256,1536]{1,0:T(8,128)(2,1)S(1)} %copy-done.25), channel_id=1, source_target_pairs={{0,1},{1,0},{2,3},{3,2},{4,5},{5,4},{6,7},{7,6},{8,9},{9,8},{10,11... | collective-permute-start | bytes 2359304 | tf_op jit(solution)/shard_map/ppermute | solution.py:472
  91.5 48.6 %collective-permute-start.16 = (bf16[256,1536]{1,0:T(8,128)(2,1)S(1)}, bf16[256,1536]{1,0:T(8,128)(2,1)S(1)}, u32[]{:S(2)}, u32[]{:S(2)}) collective-permute-start(bf16[256,1536]{1,0:T(8,128)(2,1)S(1)} %copy-done.25), channel_id=1, source_target_pairs={{0,2},{1,3},{2,0},{3,1},{4,6},{5,7},{6,4},{7,5},{8,10},{9,11},{10,... | collective-permute-start | bytes 2359304 | tf_op jit(solution)/shard_map/ppermute | solution.py:472
  92.3 47.7 %collective-permute-start.17 = (bf16[256,1536]{1,0:T(8,128)(2,1)S(1)}, bf16[256,1536]{1,0:T(8,128)(2,1)S(1)}, u32[]{:S(2)}, u32[]{:S(2)}) collective-permute-start(bf16[256,1536]{1,0:T(8,128)(2,1)S(1)} %copy-done.25), channel_id=1, source_target_pairs={{0,3},{1,2},{2,1},{3,0},{4,7},{5,6},{6,5},{7,4},{8,11},{9,10},{10,... | collective-permute-start | bytes 2359304 | tf_op jit(solution)/shard_map/ppermute | solution.py:472
  149.0 9.1 %collective-permute-start.18 = (f32[32,256]{1,0:T(8,128)}, f32[32,256]{1,0:T(8,128)S(1)}, u32[]{:S(2)}, u32[]{:S(2)}) collective-permute-start(f32[32,256]{1,0:T(8,128)} %get-tuple-element.49.refs_0_.refs_8_), channel_id=1, source_target_pairs={{0,1},{1,0},{2,3},{3,2},{4,5},{5,4},{6,7},{7,6},{8,9},{9,8},{10,11... | collective-permute-start | bytes 98312 | tf_op jit(solution)/shard_map/ppermute | solution.py:472
  150.5 7.7 %collective-permute-start.19 = (f32[32,256]{1,0:T(8,128)}, f32[32,256]{1,0:T(8,128)S(1)}, u32[]{:S(2)}, u32[]{:S(2)}) collective-permute-start(f32[32,256]{1,0:T(8,128)} %get-tuple-element.49.refs_0_.refs_8_), channel_id=1, source_target_pairs={{0,2},{1,3},{2,0},{3,1},{4,6},{5,7},{6,4},{7,5},{8,10},{9,11},{10,... | collective-permute-start | bytes 98312 | tf_op jit(solution)/shard_map/ppermute | solution.py:472
  151.3 6.9 %collective-permute-start.20 = (f32[32,256]{1,0:T(8,128)}, f32[32,256]{1,0:T(8,128)S(1)}, u32[]{:S(2)}, u32[]{:S(2)}) collective-permute-start(f32[32,256]{1,0:T(8,128)} %get-tuple-element.49.refs_0_.refs_8_), channel_id=1, source_target_pairs={{0,3},{1,2},{2,1},{3,0},{4,7},{5,6},{6,5},{7,4},{8,11},{9,10},{10,... | collective-permute-start | bytes 98312 | tf_op jit(solution)/shard_map/ppermute | solution.py:472
  166.4 48.9 %copy-start.39 = (bf16[1024,768]{1,0:T(8,128)(2,1)S(1)}, bf16[1024,768]{1,0:T(8,128)(2,1)}, u32[]{:S(2)}) copy-start(bf16[1024,768]{1,0:T(8,128)(2,1)} %get-tuple-element.52.gz_ref) | copy-start | bytes 4718596
  220.2 29.6 %collective-permute-start.29 = (bf16[4,192,768]{2,1,0:T(8,128)(2,1)S(1)}, bf16[4,192,768]{2,1,0:T(8,128)(2,1)}, u32[]{:S(2)}, u32[]{:S(2)}) collective-permute-start(bf16[4,192,768]{2,1,0:T(8,128)(2,1)S(1)} %dynamic-slice_bitcast_fusion.2), channel_id=1, source_target_pairs={{0,4},{4,0},{8,12},{12,8},{16,20},{20,16},{24,28},{28,24},{1,5},{5... | collective-permute-start | bytes 3538952 | tf_op jit(solution)/shard_map/ppermute | solution.py:472
  226.4 30.2 %collective-permute-start.37 = (bf16[4,192,768]{2,1,0:T(8,128)(2,1)}, bf16[4,192,768]{2,1,0:T(8,128)(2,1)}, u32[]{:S(2)}, u32[]{:S(2)}) collective-permute-start(bf16[4,192,768]{2,1,0:T(8,128)(2,1)} %dynamic-slice_bitcast_fusion.1), channel_id=1, source_target_pairs={{0,4},{4,0},{8,12},{12,8},{16,20},{20,16},{24,28},{28,24},{1,5},{5... | collective-permute-start | bytes 3538952 | tf_op jit(solution)/shard_map/ppermute | solution.py:472
  232.9 21.6 %collective-permute-start.53 = (bf16[384,1536]{1,0:T(8,128)(2,1)}, bf16[384,1536]{1,0:T(8,128)(2,1)}, u32[]{:S(2)}, u32[]{:S(2)}) collective-permute-start(bf16[384,1536]{1,0:T(8,128)(2,1)} %dynamic-slice_bitcast_fusion), channel_id=1, source_target_pairs={{0,4},{4,0},{8,12},{12,8},{16,20},{20,16},{24,28},{28,24},{1,5},{5... | collective-permute-start | bytes 3538952 | tf_op jit(solution)/shard_map/ppermute | solution.py:472
  248.5 13.3 %collective-permute-start.45 = (bf16[4,192,384]{2,1,0:T(8,128)(2,1)S(1)}, bf16[4,192,384]{2,1,0:T(8,128)(2,1)S(1)}, u32[]{:S(2)}, u32[]{:S(2)}) collective-permute-start(bf16[4,192,384]{2,1,0:T(8,128)(2,1)S(1)} %dynamic-slice_bitcast_fusion.3), channel_id=1, source_target_pairs={{0,4},{4,0},{8,12},{12,8},{16,20},{20,16},{24,28},{28,24},{1,5},{5... | collective-permute-start | bytes 1769480 | tf_op jit(solution)/shard_map/ppermute | solution.py:472
  251.5 12.9 %collective-permute-start.32 = (bf16[192,768]{1,0:T(8,128)(2,1)S(1)}, bf16[192,768]{1,0:T(8,128)(2,1)S(1)}, u32[]{:S(2)}, u32[]{:S(2)}) collective-permute-start(bf16[192,768]{1,0:T(8,128)(2,1)S(1)} %get-tuple-element.106), channel_id=1, source_target_pairs={{0,3},{1,2},{2,1},{3,0},{4,7},{5,6},{6,5},{7,4},{8,11},{9,10},{10,... | collective-permute-start | bytes 884744 | tf_op jit(solution)/shard_map/ppermute | solution.py:472
  253.3 14.5 %collective-permute-start.31 = (bf16[192,768]{1,0:T(8,128)(2,1)S(1)}, bf16[192,768]{1,0:T(8,128)(2,1)S(1)}, u32[]{:S(2)}, u32[]{:S(2)}) collective-permute-start(bf16[192,768]{1,0:T(8,128)(2,1)S(1)} %get-tuple-element.107), channel_id=1, source_target_pairs={{0,2},{1,3},{2,0},{3,1},{4,6},{5,7},{6,4},{7,5},{8,10},{9,11},{10,... | collective-permute-start | bytes 884744 | tf_op jit(solution)/shard_map/ppermute | solution.py:472
  254.5 15.1 %collective-permute-start.30 = (bf16[192,768]{1,0:T(8,128)(2,1)S(1)}, bf16[192,768]{1,0:T(8,128)(2,1)S(1)}, u32[]{:S(2)}, u32[]{:S(2)}) collective-permute-start(bf16[192,768]{1,0:T(8,128)(2,1)S(1)} %get-tuple-element.108), channel_id=1, source_target_pairs={{0,1},{1,0},{2,3},{3,2},{4,5},{5,4},{6,7},{7,6},{8,9},{9,8},{10,11... | collective-permute-start | bytes 884744 | tf_op jit(solution)/shard_map/ppermute | solution.py:472
  256.6 50.2 %collective-permute-start.54 = (bf16[384,1536]{1,0:T(8,128)(2,1)S(1)}, bf16[384,1536]{1,0:T(8,128)(2,1)S(1)}, u32[]{:S(2)}, u32[]{:S(2)}) collective-permute-start(bf16[384,1536]{1,0:T(8,128)(2,1)S(1)} %fusion.7), channel_id=1, source_target_pairs={{0,8},{4,12},{24,16},{28,20},{1,9},{5,13},{25,17},{29,21},{2,10},{... | collective-permute-start | bytes 3538952 | tf_op jit(solution)/shard_map/ppermute | solution.py:492
  262.9 41.8 %collective-permute-start.12 = (bf16[256,1536]{1,0:T(8,128)(2,1)S(1)}, bf16[256,1536]{1,0:T(8,128)(2,1)S(1)}, u32[]{:S(2)}, u32[]{:S(2)}) collective-permute-start(bf16[256,1536]{1,0:T(8,128)(2,1)S(1)} %copy-done.43), channel_id=1, source_target_pairs={{0,1},{1,0},{2,3},{3,2},{4,5},{5,4},{6,7},{7,6},{8,9},{9,8},{10,11... | collective-permute-start | bytes 2359304 | tf_op jit(solution)/shard_map/ppermute | solution.py:472
  264.4 41.6 %collective-permute-start.13 = (bf16[256,1536]{1,0:T(8,128)(2,1)S(1)}, bf16[256,1536]{1,0:T(8,128)(2,1)S(1)}, u32[]{:S(2)}, u32[]{:S(2)}) collective-permute-start(bf16[256,1536]{1,0:T(8,128)(2,1)S(1)} %copy-done.42), channel_id=1, source_target_pairs={{0,2},{1,3},{2,0},{3,1},{4,6},{5,7},{6,4},{7,5},{8,10},{9,11},{10,... | collective-permute-start | bytes 2359304 | tf_op jit(solution)/shard_map/ppermute | solution.py:472
  267.8 23.2 %collective-permute-start.40 = (bf16[192,768]{1,0:T(8,128)(2,1)S(1)}, bf16[192,768]{1,0:T(8,128)(2,1)S(1)}, u32[]{:S(2)}, u32[]{:S(2)}) collective-permute-start(bf16[192,768]{1,0:T(8,128)(2,1)S(1)} %get-tuple-element.102), channel_id=1, source_target_pairs={{0,3},{1,2},{2,1},{3,0},{4,7},{5,6},{6,5},{7,4},{8,11},{9,10},{10,... | collective-permute-start | bytes 884744 | tf_op jit(solution)/shard_map/ppermute | solution.py:472
  269.6 31.4 %copy-start.2 = (bf16[192,768]{1,0:T(8,128)(2,1)}, bf16[192,768]{1,0:T(8,128)(2,1)S(1)}, u32[]{:S(2)}) copy-start(bf16[192,768]{1,0:T(8,128)(2,1)S(1)} %collective-permute-done.30) | copy-start | bytes 884740
  269.6 27.6 %collective-permute-start.39 = (bf16[192,768]{1,0:T(8,128)(2,1)S(1)}, bf16[192,768]{1,0:T(8,128)(2,1)S(1)}, u32[]{:S(2)}, u32[]{:S(2)}) collective-permute-start(bf16[192,768]{1,0:T(8,128)(2,1)S(1)} %get-tuple-element.103), channel_id=1, source_target_pairs={{0,2},{1,3},{2,0},{3,1},{4,6},{5,7},{6,4},{7,5},{8,10},{9,11},{10,... | collective-permute-start | bytes 884744 | tf_op jit(solution)/shard_map/ppermute | solution.py:472
  271.5 29.4 %copy-start.38 = (f32[48]{0:T(128)}, f32[48]{0:T(128)S(1)}, u32[]{:S(2)}) copy-start(f32[48]{0:T(128)S(1)} %bitcast_dynamic-update-slice_fusion.1) | copy-start | bytes 580
  291.0 9.9 %collective-permute-start.38 = (bf16[192,768]{1,0:T(8,128)(2,1)S(1)}, bf16[192,768]{1,0:T(8,128)(2,1)S(1)}, u32[]{:S(2)}, u32[]{:S(2)}) collective-permute-start(bf16[192,768]{1,0:T(8,128)(2,1)S(1)} %get-tuple-element.104), channel_id=1, source_target_pairs={{0,1},{1,0},{2,3},{3,2},{4,5},{5,4},{6,7},{7,6},{8,9},{9,8},{10,11... | collective-permute-start | bytes 884744 | tf_op jit(solution)/shard_map/ppermute | solution.py:472
  297.2 54.5 %collective-permute-start.33 = (bf16[4,192,768]{2,1,0:T(8,128)(2,1)}, bf16[4,192,768]{2,1,0:T(8,128)(2,1)S(1)}, u32[]{:S(2)}, u32[]{:S(2)}) collective-permute-start(bf16[4,192,768]{2,1,0:T(8,128)(2,1)} %pad_maximum_fusion.1), channel_id=1, source_target_pairs={{0,8},{4,12},{24,16},{28,20},{1,9},{5,13},{25,17},{29,21},{2,10},{... | collective-permute-start | bytes 3538952 | tf_op jit(solution)/shard_map/ppermute | solution.py:492
  301.0 21.5 %collective-permute-start.14 = (bf16[256,1536]{1,0:T(8,128)(2,1)S(1)}, bf16[256,1536]{1,0:T(8,128)(2,1)S(1)}, u32[]{:S(2)}, u32[]{:S(2)}) collective-permute-start(bf16[256,1536]{1,0:T(8,128)(2,1)S(1)} %copy-done.41), channel_id=1, source_target_pairs={{0,3},{1,2},{2,1},{3,0},{4,7},{5,6},{6,5},{7,4},{8,11},{9,10},{10,... | collective-permute-start | bytes 2359304 | tf_op jit(solution)/shard_map/ppermute | solution.py:472
  304.7 25.7 %collective-permute-start.48 = (bf16[192,384]{1,0:T(8,128)(2,1)}, bf16[192,384]{1,0:T(8,128)(2,1)}, u32[]{:S(2)}, u32[]{:S(2)}) collective-permute-start(bf16[192,384]{1,0:T(8,128)(2,1)} %get-tuple-element.110), channel_id=1, source_target_pairs={{0,3},{1,2},{2,1},{3,0},{4,7},{5,6},{6,5},{7,4},{8,11},{9,10},{10,... | collective-permute-start | bytes 442376 | tf_op jit(solution)/shard_map/ppermute | solution.py:472
  306.0 25.5 %collective-permute-start.47 = (bf16[192,384]{1,0:T(8,128)(2,1)}, bf16[192,384]{1,0:T(8,128)(2,1)}, u32[]{:S(2)}, u32[]{:S(2)}) collective-permute-start(bf16[192,384]{1,0:T(8,128)(2,1)} %get-tuple-element.111), channel_id=1, source_target_pairs={{0,2},{1,3},{2,0},{3,1},{4,6},{5,7},{6,4},{7,5},{8,10},{9,11},{10,... | collective-permute-start | bytes 442376 | tf_op jit(solution)/shard_map/ppermute | solution.py:472
  306.9 48.1 %collective-permute-start.41 = (bf16[4,192,768]{2,1,0:T(8,128)(2,1)}, bf16[4,192,768]{2,1,0:T(8,128)(2,1)}, u32[]{:S(2)}, u32[]{:S(2)}) collective-permute-start(bf16[4,192,768]{2,1,0:T(8,128)(2,1)} %pad_maximum_fusion.2), channel_id=1, source_target_pairs={{0,8},{4,12},{24,16},{28,20},{1,9},{5,13},{25,17},{29,21},{2,10},{... | collective-permute-start | bytes 3538952 | tf_op jit(solution)/shard_map/ppermute | solution.py:492
  323.4 73.4 %collective-permute-start.55 = (bf16[384,1536]{1,0:T(8,128)(2,1)S(1)}, bf16[384,1536]{1,0:T(8,128)(2,1)}, u32[]{:S(2)}, u32[]{:S(2)}) collective-permute-start(bf16[384,1536]{1,0:T(8,128)(2,1)S(1)} %add_convert_fusion.1), channel_id=1, source_target_pairs={{8,16},{12,20},{16,8},{20,12},{9,17},{13,21},{17,9},{21,13},{10,18... | collective-permute-start | bytes 3538952 | tf_op jit(solution)/shard_map/ppermute | solution.py:493
  330.4 28.9 %collective-permute-start.21 = (bf16[256,1536]{1,0:T(8,128)(2,1)}, bf16[256,1536]{1,0:T(8,128)(2,1)}, u32[]{:S(2)}, u32[]{:S(2)}) collective-permute-start(bf16[256,1536]{1,0:T(8,128)(2,1)} %get-tuple-element.58), channel_id=1, source_target_pairs={{0,1},{1,0},{2,3},{3,2},{4,5},{5,4},{6,7},{7,6},{8,9},{9,8},{10,11... | collective-permute-start | bytes 2359304 | tf_op jit(solution)/shard_map/ppermute | solution.py:472
  331.6 19.3 %collective-permute-start.46 = (bf16[192,384]{1,0:T(8,128)(2,1)}, bf16[192,384]{1,0:T(8,128)(2,1)S(1)}, u32[]{:S(2)}, u32[]{:S(2)}) collective-permute-start(bf16[192,384]{1,0:T(8,128)(2,1)} %get-tuple-element.109), channel_id=1, source_target_pairs={{0,1},{1,0},{2,3},{3,2},{4,5},{5,4},{6,7},{7,6},{8,9},{9,8},{10,11... | collective-permute-start | bytes 442376 | tf_op jit(solution)/shard_map/ppermute | solution.py:472
  350.9 33.5 %collective-permute-start.22 = (bf16[256,1536]{1,0:T(8,128)(2,1)}, bf16[256,1536]{1,0:T(8,128)(2,1)}, u32[]{:S(2)}, u32[]{:S(2)}) collective-permute-start(bf16[256,1536]{1,0:T(8,128)(2,1)} %get-tuple-element.59), channel_id=1, source_target_pairs={{0,2},{1,3},{2,0},{3,1},{4,6},{5,7},{6,4},{7,5},{8,10},{9,11},{10,... | collective-permute-start | bytes 2359304 | tf_op jit(solution)/shard_map/ppermute | solution.py:472
  351.7 36.0 %collective-permute-start.23 = (bf16[256,1536]{1,0:T(8,128)(2,1)}, bf16[256,1536]{1,0:T(8,128)(2,1)}, u32[]{:S(2)}, u32[]{:S(2)}) collective-permute-start(bf16[256,1536]{1,0:T(8,128)(2,1)} %get-tuple-element.60), channel_id=1, source_target_pairs={{0,3},{1,2},{2,1},{3,0},{4,7},{5,6},{6,5},{7,4},{8,11},{9,10},{10,... | collective-permute-start | bytes 2359304 | tf_op jit(solution)/shard_map/ppermute | solution.py:472
  355.0 44.7 %collective-permute-start.34 = (bf16[4,192,768]{2,1,0:T(8,128)(2,1)}, bf16[4,192,768]{2,1,0:T(8,128)(2,1)}, u32[]{:S(2)}, u32[]{:S(2)}) collective-permute-start(bf16[4,192,768]{2,1,0:T(8,128)(2,1)} %add_convert_fusion.5), channel_id=1, source_target_pairs={{8,16},{12,20},{16,8},{20,12},{9,17},{13,21},{17,9},{21,13},{10,18... | collective-permute-start | bytes 3538952 | tf_op jit(solution)/shard_map/ppermute | solution.py:493
  359.3 43.5 %collective-permute-start.42 = (bf16[4,192,768]{2,1,0:T(8,128)(2,1)}, bf16[4,192,768]{2,1,0:T(8,128)(2,1)}, u32[]{:S(2)}, u32[]{:S(2)}) collective-permute-start(bf16[4,192,768]{2,1,0:T(8,128)(2,1)} %add_convert_fusion.3), channel_id=1, source_target_pairs={{8,16},{12,20},{16,8},{20,12},{9,17},{13,21},{17,9},{21,13},{10,18... | collective-permute-start | bytes 3538952 | tf_op jit(solution)/shard_map/ppermute | solution.py:493
  384.3 27.9 %collective-permute-start.49 = (bf16[192,384]{1,0:T(8,128)(2,1)}, bf16[192,384]{1,0:T(8,128)(2,1)}, u32[]{:S(2)}, u32[]{:S(2)}) collective-permute-start(bf16[192,384]{1,0:T(8,128)(2,1)} %fusion.13), channel_id=1, source_target_pairs={{0,8},{4,12},{24,16},{28,20},{1,9},{5,13},{25,17},{29,21},{2,10},{... | collective-permute-start | bytes 442376 | tf_op jit(solution)/shard_map/ppermute | solution.py:492
  398.3 30.7 %collective-permute-start.56 = (bf16[384,1536]{1,0:T(8,128)(2,1)S(1)}, bf16[384,1536]{1,0:T(8,128)(2,1)S(1)}, u32[]{:S(2)}, u32[]{:S(2)}) collective-permute-start(bf16[384,1536]{1,0:T(8,128)(2,1)S(1)} %add_convert_fusion), channel_id=1, source_target_pairs={{8,0},{12,4},{16,24},{20,28},{9,1},{13,5},{17,25},{21,29},{10,2},{... | collective-permute-start | bytes 3538952 | tf_op jit(solution)/shard_map/ppermute | solution.py:494
  399.7 6.6 %collective-permute-start.24 = (f32[168,128]{1,0:T(8,128)S(1)}, f32[168,128]{1,0:T(8,128)S(1)}, u32[]{:S(2)}, u32[]{:S(2)}) collective-permute-start(f32[168,128]{1,0:T(8,128)S(1)} %pad_bitcast_fusion), channel_id=1, source_target_pairs={{0,4},{4,0},{8,12},{12,8},{16,20},{20,16},{24,28},{28,24},{1,5},{5... | collective-permute-start | bytes 258056 | tf_op jit(solution)/shard_map/ppermute | solution.py:472
  401.6 52.8 %collective-permute-start.35 = (bf16[4,192,768]{2,1,0:T(8,128)(2,1)S(1)}, bf16[4,192,768]{2,1,0:T(8,128)(2,1)S(1)}, u32[]{:S(2)}, u32[]{:S(2)}) collective-permute-start(bf16[4,192,768]{2,1,0:T(8,128)(2,1)S(1)} %add_convert_fusion.4), channel_id=1, source_target_pairs={{8,0},{12,4},{16,24},{20,28},{9,1},{13,5},{17,25},{21,29},{10,2},{... | collective-permute-start | bytes 3538952 | tf_op jit(solution)/shard_map/ppermute | solution.py:494
  405.0 72.8 %collective-permute-start.43 = (bf16[4,192,768]{2,1,0:T(8,128)(2,1)S(1)}, bf16[4,192,768]{2,1,0:T(8,128)(2,1)S(1)}, u32[]{:S(2)}, u32[]{:S(2)}) collective-permute-start(bf16[4,192,768]{2,1,0:T(8,128)(2,1)S(1)} %add_convert_fusion.2), channel_id=1, source_target_pairs={{8,0},{12,4},{16,24},{20,28},{9,1},{13,5},{17,25},{21,29},{10,2},{... | collective-permute-start | bytes 3538952 | tf_op jit(solution)/shard_map/ppermute | solution.py:494
  406.3 72.4 %collective-permute-start.25 = (f32[168,128]{1,0:T(8,128)S(1)}, f32[168,128]{1,0:T(8,128)S(1)}, u32[]{:S(2)}, u32[]{:S(2)}) collective-permute-start(f32[168,128]{1,0:T(8,128)S(1)} %fusion.18), channel_id=1, source_target_pairs={{0,8},{4,12},{8,0},{12,4},{16,24},{20,28},{24,16},{28,20},{1,9},{5... | collective-permute-start | bytes 258056 | tf_op jit(solution)/shard_map/ppermute | solution.py:472
  413.3 65.5 %collective-permute-start.50 = (bf16[192,384]{1,0:T(8,128)(2,1)S(1)}, bf16[192,384]{1,0:T(8,128)(2,1)S(1)}, u32[]{:S(2)}, u32[]{:S(2)}) collective-permute-start(bf16[192,384]{1,0:T(8,128)(2,1)S(1)} %add_convert_fusion.7), channel_id=1, source_target_pairs={{8,16},{12,20},{16,8},{20,12},{9,17},{13,21},{17,9},{21,13},{10,18... | collective-permute-start | bytes 442376 | tf_op jit(solution)/shard_map/ppermute | solution.py:493
  429.2 26.3 %copy-start = (bf16[384,1536]{1,0:T(8,128)(2,1)}, bf16[384,1536]{1,0:T(8,128)(2,1)S(1)}, u32[]{:S(2)}) copy-start(bf16[384,1536]{1,0:T(8,128)(2,1)S(1)} %broadcast_select_fusion.ok) | copy-start | bytes 3538948
  429.2 74.4 %collective-permute-start.57 = (bf16[384,1536]{1,0:T(8,128)(2,1)S(1)}, bf16[384,1536]{1,0:T(8,128)(2,1)S(1)}, u32[]{:S(2)}, u32[]{:S(2)}) collective-permute-start(bf16[384,1536]{1,0:T(8,128)(2,1)S(1)} %broadcast_select_fusion.ok), channel_id=1, source_target_pairs={{0,4},{4,0},{8,12},{12,8},{16,20},{20,16},{24,28},{28,24},{1,5},{5... | collective-permute-start | bytes 3538952 | tf_op jit(solution)/shard_map/ppermute | solution.py:472
  455.5 48.1 %collective-permute-start.36 = (bf16[4,192,768]{2,1,0:T(8,128)(2,1)}, bf16[4,192,768]{2,1,0:T(8,128)(2,1)}, u32[]{:S(2)}, u32[]{:S(2)}) collective-permute-start(bf16[4,192,768]{2,1,0:T(8,128)(2,1)} %broadcast_select_fusion.2.zk), channel_id=1, source_target_pairs={{0,4},{4,0},{8,12},{12,8},{16,20},{20,16},{24,28},{28,24},{1,5},{5... | collective-permute-start | bytes 3538952 | tf_op jit(solution)/shard_map/ppermute | solution.py:472
  477.9 25.7 %collective-permute-start.44 = (bf16[4,192,768]{2,1,0:T(8,128)(2,1)S(1)}, bf16[4,192,768]{2,1,0:T(8,128)(2,1)}, u32[]{:S(2)}, u32[]{:S(2)}) collective-permute-start(bf16[4,192,768]{2,1,0:T(8,128)(2,1)S(1)} %broadcast_select_fusion.1.vk), channel_id=1, source_target_pairs={{0,4},{4,0},{8,12},{12,8},{16,20},{20,16},{24,28},{28,24},{1,5},{5... | collective-permute-start | bytes 3538952 | tf_op jit(solution)/shard_map/ppermute | solution.py:472
  478.7 6.2 %collective-permute-start.26 = (f32[168,128]{1,0:T(8,128)S(1)}, f32[168,128]{1,0:T(8,128)S(1)}, u32[]{:S(2)}, u32[]{:S(2)}) collective-permute-start(f32[168,128]{1,0:T(8,128)S(1)} %fusion.28), channel_id=1, source_target_pairs={{0,16},{4,20},{8,24},{12,28},{16,0},{20,4},{24,8},{28,12},{1,17},{... | collective-permute-start | bytes 258056 | tf_op jit(solution)/shard_map/ppermute | solution.py:472
  479.5 12.6 %collective-permute-start.51 = (bf16[192,384]{1,0:T(8,128)(2,1)}, bf16[192,384]{1,0:T(8,128)(2,1)}, u32[]{:S(2)}, u32[]{:S(2)}) collective-permute-start(bf16[192,384]{1,0:T(8,128)(2,1)} %add_convert_fusion.6), channel_id=1, source_target_pairs={{8,0},{12,4},{16,24},{20,28},{9,1},{13,5},{17,25},{21,29},{10,2},{... | collective-permute-start | bytes 442376 | tf_op jit(solution)/shard_map/ppermute | solution.py:494
  485.6 4.8 collective-permute-start.27
  491.3 4.6 collective-permute-start.28
  493.7 9.9 %collective-permute-start.52 = (bf16[192,384]{1,0:T(8,128)(2,1)}, bf16[192,384]{1,0:T(8,128)(2,1)}, u32[]{:S(2)}, u32[]{:S(2)}) collective-permute-start(bf16[192,384]{1,0:T(8,128)(2,1)} %broadcast_select_fusion.3.sk), channel_id=1, source_target_pairs={{0,4},{4,0},{8,12},{12,8},{16,20},{20,16},{24,28},{28,24},{1,5},{5... | collective-permute-start | bytes 442376 | tf_op jit(solution)/shard_map/ppermute | solution.py:472
  (53 other events, 174.9 us)
